TPU v7x, 256 devices: a whole 4x4x8 slice. The times are simulated.
256 devices in a mesh: row: 32 (over z, y_lo, core), col: 8 (over y_hi, x).
Axes of the slice: x: 4, y: 4 (y_hi: 2, y_lo: 2; y = y_hi * 2 + y_lo), z: 8, core: 2. Of those that a mesh axis runs over, the one named last changes fastest.
Arguments:
- matrix: float32 [14336, 14336], P('row', 'col'), may hold values from -16 to 16, as said below
- panels: float32 [2, 14336, 128], P(None, 'row'), may hold values from -0.050111484 to 0.050111484
- factors: float32 [2, 128, 128], replicated, may hold values from -1.2 to 1.6, as said below
Outputs:
- updated: float32 [14336, 14336], P('row', 'col')
Inputs may be any that keep to these rules, and one draw needn't show every extreme that they name: symmetric: matrix[r, c] equals matrix[c, r]. Each factors[p] is upper triangular, with diagonal entries between 0.8 and 1.6.
All inputs are finite; a program needn't handle non-finite values.
Results may differ from a plain program's by a relative error of at most 0.0001.
Values sent between devices are 32-bit elements; how exact they have to be, the bound alone decides.
A program may use at most 64 MiB of HBM per device.

v0:
```python
import jax
import jax.numpy as jnp
from jax import lax
from jax.sharding import PartitionSpec as P


def matmul(former, latter):
    return jnp.dot(former, latter, precision=lax.Precision.HIGHEST)


def transposed_dot(former, latter):
    return lax.dot_general(
        former, latter, (((0,), (0,)), ((), ())), precision=lax.Precision.HIGHEST
    )


def outer_drop(current, former, latter):
    return current - lax.dot_general(
        former, latter, (((1,), (1,)), ((), ())), precision=lax.Precision.HIGHEST
    )


def weights(forward, vectors, factor, correct):
    return matmul(forward, factor) - 0.5 * matmul(vectors, correct)


def row_sums(current, vector_rows, extra_terms):
    summed = lax.psum((transposed_dot(current, vector_rows),) + extra_terms, "row")
    return (summed[0], tuple(summed[1:]))


def shards(matrix, panels, factors):
    col_index = lax.axis_index("col")
    local_cols = matrix.shape[1]
    gathered = lax.all_gather(panels, "row", axis=1, tiled=True)
    vector_cols = lax.dynamic_slice_in_dim(gathered, col_index * local_cols, local_cols, 1)
    current = matrix
    for number in range(panels.shape[0]):
        vector_rows = panels[number]
        vcol_now = vector_cols[number]
        factor = factors[number]
        forward = lax.psum(matmul(current, vcol_now), "col")
        forward_cols, summed = row_sums(
            current, vector_rows, (transposed_dot(vector_rows, forward),)
        )
        correct = matmul(factor.T, matmul(summed[0], factor))
        wrow_now = weights(forward, vector_rows, factor, correct)
        wcol_now = weights(forward_cols, vcol_now, factor, correct)
        current = outer_drop(
            current,
            jnp.concatenate([vector_rows, wrow_now], axis=1),
            jnp.concatenate([wcol_now, vcol_now], axis=1),
        )
    return current


def solution(mesh):
    placed = (P("row", "col"), P(None, "row", None), P())
    return jax.shard_map(
        shards, mesh=mesh, in_specs=placed, out_specs=P("row", "col"), check_vma=False
    )
```

profile of v0, /device:TPU:1, one launch (start us, length us, event | category | flops | bytes accessed | tf_op | source)
XLA Modules:
  0.0 775.0 jit_solution(1958344349460214117)
XLA Ops:
  6.5 0.7 all-gather.2.cloned.1.call-update
  7.3 95.2 %all-gather.2.cloned.1.call-done = f32[2,14336,128]{2,1,0:T(8,128)} async-done(((f32[2,448,128]{2,1,0:T(8,128)}), f32[2,14336,128]{2,1,0:T(8,128)}) %all-gather.2.cloned.1.call-update) | async-done | bytes 14680080 | tf_op jit(solution)/shard_map/all_gather | solution.py:35
  102.5 2.5 dynamic-slice_bitcast_fusion
  105.0 0.9 copy-done.3
  105.9 3.4 convolution_bitcast_fusion
  109.3 0.0 all-reduce.13.cloned.1.call-start
  109.4 7.8 %fusion.44 = f32[1792,128]{1,0:T(8,128)} fusion(f32[448,1792]{1,0:T(8,128)S(1)} %copy-done, f32[2,448,128]{2,1,0:T(8,128)} %param.4), kind=kOutput, calls=%fused_computation.57 | convolution fusion | flops 1233125376 | bytes 4358144 | tf_op jit(solution)/shard_map/dot_general | solution.py:12
  117.2 74.7 %all-reduce.7.cloned.1.call-done = f32[448,128]{1,0:T(8,128)} async-done(((f32[448,128]{1,0:T(8,128)}), f32[448,128]{1,0:T(8,128)}) %all-reduce.7.cloned.1.call-update) | async-done | bytes 229392 | tf_op jit(solution)/shard_map/psum | solution.py:42
  191.9 2.3 convolution_bitcast_fusion.2
  194.2 0.2 all-reduce.9.cloned.1.call-start
  194.4 1.9 slice_bitcast_fusion
  196.3 1.3 fusion.32
  197.6 228.8 %all-reduce.13.cloned.1.call-done = (f32[1792,128]{1,0:T(8,128)}, f32[128,128]{0,1:T(8,128)}) async-done(((f32[1792,128]{1,0:T(8,128)}, f32[128,128]{0,1:T(8,128)}), (f32[1792,128]{1,0:T(8,128)}, f32[128,128]{0,1:T(8,128)})) %all-reduce.13.cloned.1.call-update) | async-done | bytes 983056 | tf_op jit(solution)/shard_map/psum | solution.py:28
  426.3 2.1 fusion.26
  428.4 1.1 fusion.30
  429.6 0.3 fusion.28
  429.9 0.9 fusion.1
  430.8 0.4 fusion.11
  431.2 5.1 convolution_subtract_fusion.1
  436.3 3.4 fusion.46
  439.7 0.3 all-reduce.11.cloned.1.call-start
  439.9 7.8 %fusion.45 = f32[1792,128]{1,0:T(8,128)} fusion(f32[448,1792]{1,0:T(8,128)S(1)} %convolution_subtract_fusion.1, f32[2,448,128]{2,1,0:T(8,128)} %param.4), kind=kOutput, calls=%fused_computation.58 | convolution fusion | flops 1233125376 | bytes 4358144 | tf_op jit(solution)/shard_map/dot_general | solution.py:12
  447.7 75.9 %all-reduce.9.cloned.1.call-done = f32[448,128]{1,0:T(8,128)} async-done(((f32[448,128]{1,0:T(8,128)}), f32[448,128]{1,0:T(8,128)}) %all-reduce.9.cloned.1.call-update) | async-done | bytes 229392 | tf_op jit(solution)/shard_map/psum | solution.py:42
  523.6 2.3 convolution_bitcast_fusion.1
  525.9 2.0 fusion.24
  527.9 230.0 %all-reduce.11.cloned.1.call-done = (f32[1792,128]{1,0:T(8,128)}, f32[128,128]{0,1:T(8,128)}) async-done(((f32[1792,128]{1,0:T(8,128)}, f32[128,128]{0,1:T(8,128)}), (f32[1792,128]{1,0:T(8,128)}, f32[128,128]{0,1:T(8,128)})) %all-reduce.11.cloned.1.call-update) | async-done | bytes 983056 | tf_op jit(solution)/shard_map/psum | solution.py:28
  757.9 2.2 fusion.18
  760.1 1.1 fusion.22
  761.2 0.3 fusion.20
  761.5 2.1 fusion
  763.6 0.4 fusion.9
  764.0 4.5 convolution_subtract_fusion
  (27 shorter events, 0.2 us)
Async XLA Ops:
  6.5 99.4 %copy-start = (f32[448,1792]{1,0:T(8,128)S(1)}, f32[448,1792]{1,0:T(8,128)}, u32[]{:S(2)}) copy-start(f32[448,1792]{1,0:T(8,128)} %param.3) | copy-start | bytes 9633796
  6.5 96.0 %all-gather.2.cloned.1.call-start = ((), (), s32[]{:S(2)}) async-start(), calls=%async_computation | async-start | bytes 15138816 | tf_op jit(solution)/shard_map/all_gather | solution.py:35
  7.3 184.6 %all-reduce.7.cloned.1.call-start = ((), (), s32[]{:S(2)}) async-start(), calls=%async_computation.1 | async-start | bytes 458752 | tf_op jit(solution)/shard_map/psum | solution.py:42
  105.0 0.9 copy-start.3
  109.3 87.0 %copy-start.7 = (f32[2,128,128]{2,1,0:T(8,128)S(1)}, f32[2,128,128]{2,1,0:T(8,128)}, u32[]{:S(2)}) copy-start(f32[2,128,128]{2,1,0:T(8,128)} %param.5) | copy-start | bytes 393220
  109.3 317.0 %all-reduce.13.cloned.1.call-start = ((), (), s32[]{:S(2)}) async-start(), calls=%async_computation.4 | async-start | bytes 1966080 | tf_op jit(solution)/shard_map/psum | solution.py:28
  117.2 312.7 %copy-start.4 = (f32[1792,128]{1,0:T(8,128)S(1)}, f32[1792,128]{1,0:T(8,128)}, u32[]{:S(2)}) copy-start(f32[1792,128]{1,0:T(8,128)} %copy-done.3) | copy-start | bytes 2752516
  194.2 236.6 %copy-start.5 = (f32[2,448,128]{2,1,0:T(8,128)S(1)}, f32[2,448,128]{2,1,0:T(8,128)}, u32[]{:S(2)}) copy-start(f32[2,448,128]{2,1,0:T(8,128)} %param.4) | copy-start | bytes 1376260
  194.2 329.4 %all-reduce.9.cloned.1.call-start = ((), (), s32[]{:S(2)}) async-start(), calls=%async_computation.2 | async-start | bytes 458752 | tf_op jit(solution)/shard_map/psum | solution.py:42
  426.3 4.8 copy-start.9
  431.2 5.1 copy-start.1
  439.7 318.2 %all-reduce.11.cloned.1.call-start = ((), (), s32[]{:S(2)}) async-start(), calls=%async_computation.3 | async-start | bytes 1966080 | tf_op jit(solution)/shard_map/psum | solution.py:28
  757.9 5.7 copy-start.6
  757.9 5.7 copy-start.10
  757.9 6.1 copy-start.2
  757.9 6.1 copy-start.8
Sparse Core Ops, SparseCore 0:
  9.1 93.3 all-gather.1
  109.4 82.4 all-reduce.6
  194.6 231.7 all-reduce.12
  439.8 83.7 all-reduce.8
  526.2 231.7 all-reduce.10
where the time goes:
time: 775 us
  waiting for transfers between devices  705 us (91%)
  matrix products  50.4 us (7%)
  between operations  13.3 us (2%)
    psum x2, waiting for transfers between devices, row_sums(): lax.psum((transposed_dot(current, vector_rows),) + extra_terms, 'row')  459 us
    psum x2, waiting for transfers between devices, shards(): forward = lax.psum(matmul(current, vcol_now), 'col')  151 us
    all_gather x1, waiting for transfers between devices, shards(): gathered = lax.all_gather(panels, 'row', axis=1, tiled=True)  95.2 us
    dot_general x14, matrix products, matmul(): return jnp.dot(former, latter, precision=lax.Precision.HIGHEST)  20.8 us
    dot_general x4, matrix products, transposed_dot(): lax.dot_general(former, latter, (((0,), (0,)), ((), ())), precision=lax.P...  20.1 us
  transfers between devices with their start and end apart: 5, of which 5 were waited for; matrix products, arithmetic and copies ran while one was open for 3% of the time, Pallas kernels for 0%

commit v1 on v0

v1 whole, which is shorter than its diff:
```python
import functools

import jax
import jax.numpy as jnp
from jax import lax
from jax.experimental import pallas as pl
from jax.experimental.pallas import tpu as pltpu
from jax.sharding import PartitionSpec as P

MESH = pl.DeviceIdType.MESH
F32 = jnp.float32
BF16 = jnp.bfloat16
NN = (((1,), (0,)), ((), ()))
NT = (((1,), (1,)), ((), ()))
TN = (((0,), (0,)), ((), ()))


def exact(a, b, dims=NN):
    return lax.dot_general(
        a, b, dims, precision=lax.Precision.HIGHEST, preferred_element_type=F32
    )


def halves(value):
    high = value.astype(BF16)
    return high, (value - high.astype(F32)).astype(BF16)


def dot3(a, b, dims=NN):
    (ah, al), (bh, bl) = a, b

    def one(p, q):
        return lax.dot_general(p, q, dims, preferred_element_type=F32)

    return one(ah, bh) + (one(ah, bl) + one(al, bh))


def exchange(nz, a_hbm, v_ref, f_ref, yc, vc, lh, ll,
             a_buf, v1, p_buf, rs, y1, yr, sp, srs, sf,
             a_sem, own_sem, g_send, g1_recv, g2_recv, g3_recv,
             rs_send, rs_recv, ag_send, ag_recv, ss_send, ss_recv, sg_send, sg_recv):
    row, col = lax.axis_index("row"), lax.axis_index("col")
    z, quad = row // 4, row % 4
    yl, core = quad // 2, quad % 2
    rows, width = a_buf.shape
    piece = rows // nz
    plane = 4 * nz
    srows = sp.shape[0] // plane
    mine = col * 4 + quad

    def at(ref, index, size):
        return ref.at[:, pl.ds(pl.multiple_of(index * size, 8), size), :]

    def send(src, dst, ssem, rsem, to_row, to_col):
        pltpu.make_async_remote_copy(
            src_ref=src, dst_ref=dst, send_sem=ssem, recv_sem=rsem,
            device_id=(to_row, to_col), device_id_type=MESH,
        ).start()

    def drain(ref, sem):
        pltpu.make_async_copy(ref, ref, sem).wait()

    load = pltpu.make_async_copy(a_hbm, a_buf, a_sem)
    load.start()
    own = pltpu.make_async_copy(at(v_ref, col, piece), at(v1, z, piece), own_sem)
    own.start()

    def zpeer(step):
        return (z + step) % nz

    def ppeer(step):
        other = (mine + step) % plane
        return z * 4 + other % 4, other // 4

    barrier = pltpu.get_barrier_semaphore()

    def greet_z(step, carry):
        pl.semaphore_signal(barrier, inc=1, device_id=(zpeer(step) * 4 + quad, col), device_id_type=MESH)
        return carry

    def greet_plane(step, carry):
        pl.semaphore_signal(barrier, inc=1, device_id=ppeer(step), device_id_type=MESH)
        return carry

    lax.fori_loop(1, nz, greet_z, 0)
    lax.fori_loop(1, plane, greet_plane, 0)
    pl.semaphore_wait(barrier, nz - 1 + plane - 1)

    def zorder(index):
        return (z + ((index % 2) * 2 - 1) * ((index + 1) // 2) + nz) % nz

    def spread(src, dst, which):
        def body(index, carry):
            to = zorder(nz - 1 - index)
            send(src, at(dst, z, piece), g_send.at[which, 0], g1_recv.at[which, z], to * 4 + quad, col)
            return carry

        lax.fori_loop(0, nz - 1, body, 0)

    def deliver(held, full, which):
        def body(index, carry):
            target = zorder(index)
            src = at(held, target, piece)

            @pl.when(index > 0)
            def _():
                drain(src, g1_recv.at[which, target])

            dst = full.at[:, pl.ds(pl.multiple_of(quad * rows + col * piece, 8), piece), :]

            send(src, dst, g_send.at[which, 1], g2_recv.at[which, yl], z * 4 + (1 - yl) * 2 + core, target)

            @pl.when(target != col)
            def _():
                send(src, dst, g_send.at[which, 2], g2_recv.at[which, yl], row, target)

            @pl.when(target == col)
            def _():
                pltpu.make_async_copy(src, dst, g2_recv.at[which, yl]).start()

            return carry

        lax.fori_loop(0, nz, body, 0)

    def relay(full, which):
        for side in range(2):
            block = at(full, side * 2 + core, rows)
            drain(block, g2_recv.at[which, side])
            send(block, block, g_send.at[which, 3 + side], g3_recv.at[which, side], z * 4 + yl * 2 + (1 - core), col)

    def partner(full, which, side):
        drain(at(full, side * 2 + (1 - core), rows), g3_recv.at[which, side])

    def settle(held, full, which):
        drain(at(held, 0, (nz - 1) * piece), g_send.at[which, 0])
        drain(at(held, 0, nz * piece), g_send.at[which, 1])
        drain(at(held, 0, (nz - 1) * piece), g_send.at[which, 2])
        for side in range(2):
            drain(at(full, 0, rows), g_send.at[which, 3 + side])

    own.wait()
    spread(at(v1, z, piece), v1, 0)
    deliver(v1, vc, 0)
    relay(vc, 0)
    load.wait()

    for side in range(2):
        partner(vc, 0, side)
        span = slice(side * 2 * rows, (side + 1) * 2 * rows)
        left = halves(a_buf[:, span])
        for panel in range(2):
            part = dot3(left, halves(vc[panel, span, :]))
            if side == 0:
                p_buf[panel] = part
            else:
                p_buf[panel] = p_buf[panel] + part

    def scatter(step, carry):
        to = (col + step) % nz
        send(at(p_buf, to, piece), at(rs, col, piece), rs_send, rs_recv, row, to)
        return carry

    lax.fori_loop(1, nz, scatter, 0)
    mine_rows = pl.ds(pl.multiple_of(col * piece, 8), piece)
    rs[:, mine_rows, :] = p_buf[:, mine_rows, :]
    drain(at(rs, 0, (nz - 1) * piece), rs_recv)
    total = rs[:, 0:piece, :]
    for other in range(1, nz):
        total = total + rs[:, other * piece:(other + 1) * piece, :]
    z_rows = pl.ds(pl.multiple_of(z * piece, 8), piece)
    y1[:, z_rows, :] = total
    yr[:, mine_rows, :] = total

    spread(at(y1, z, piece), y1, 1)

    def gather(step, carry):
        to = (col + step) % nz
        send(at(yr, col, piece), at(yr, col, piece), ag_send, ag_recv, row, to)
        return carry

    lax.fori_loop(1, nz, gather, 0)
    deliver(y1, yc, 1)

    half = sp.shape[0] // 2
    sp[:half, :half] = exact(v1[0], y1[0], TN)
    sp[:half, half:] = exact(v1[0], y1[1], TN)
    sp[half:, :half] = exact(v1[0], v1[1], TN)
    sp[half:, half:] = exact(v1[1], y1[1], TN)

    def split_sum(step, carry):
        to_row, to_col = ppeer(step)
        other = (mine + step) % plane
        send(sp.at[pl.ds(pl.multiple_of(other * srows, 8), srows), :], srs.at[mine], ss_send, ss_recv, to_row, to_col)
        return carry

    lax.fori_loop(1, plane, split_sum, 0)
    s_rows = pl.ds(pl.multiple_of(mine * srows, 8), srows)
    srs[mine] = sp[s_rows, :]
    relay(yc, 1)
    drain(srs.at[0:plane - 1], ss_recv)
    sf[s_rows, :] = jnp.sum(srs[...], axis=0)

    def join_sum(step, carry):
        to_row, to_col = ppeer(step)
        part = sf.at[s_rows, :]
        send(part, part, sg_send, sg_recv, to_row, to_col)
        return carry

    lax.fori_loop(1, plane, join_sum, 0)
    drain(at(yr, 0, (nz - 1) * piece), ag_recv)
    drain(sf.at[0:(plane - 1) * srows, :], sg_recv)

    f1, f2 = f_ref[0], f_ref[1]
    s11, s12 = sf[:half, :half], sf[:half, half:]
    gram, s22 = sf[half:, :half], sf[half:, half:]
    k1 = exact(exact(f1, s11, TN), f1)
    fs = exact(f1, s12, TN)
    kg = exact(k1, gram)
    mixed = exact(kg - fs, f2)
    cross = fs - 0.5 * kg
    gt = exact(gram, cross, TN)
    k2 = exact(exact(f2, s22 - gt - gt.T, TN), f2)
    e = exact(exact(f1, gram), f2)

    va, vb = v_ref[0], v_ref[1]
    ya, yb = yr[0], yr[1]
    parts = (
        exact(va, f1, NT) - exact(vb, e, NT),
        exact(vb, f2, NT),
        exact(ya, f1) - exact(va, k1) + exact(vb, mixed, NT),
        exact(yb, f2) - exact(ya, e) + exact(va, mixed) - exact(vb, k2),
    )
    for index, part in enumerate(parts):
        high, low = halves(part)
        lh[:, index * half:(index + 1) * half] = high
        ll[:, index * half:(index + 1) * half] = low

    for side in range(2):
        partner(yc, 1, side)
    settle(v1, vc, 0)
    settle(y1, yc, 1)
    drain(at(rs, 0, (nz - 1) * piece), rs_send)
    drain(at(rs, 0, (nz - 1) * piece), ag_send)
    drain(srs.at[0:plane - 1], ss_send)
    drain(srs.at[0:plane - 1], sg_send)


def apply_update(a_ref, yc, vc, lh, ll, out):
    right = jnp.concatenate([yc[0], yc[1], vc[0], vc[1]], axis=1)
    out[...] = a_ref[...] - dot3((lh[...], ll[...]), halves(right), NT)


def shards(nz, matrix, panels, factors):
    rows, width = matrix.shape
    size = panels.shape[2]
    piece = rows // nz
    srows = 2 * size // (4 * nz)
    vmem = pl.BlockSpec(memory_space=pltpu.VMEM)
    wide = jax.ShapeDtypeStruct((2, width, size), F32)
    left = jax.ShapeDtypeStruct((rows, 4 * size), BF16)
    block = pltpu.VMEM((2, rows, size), F32)
    dma = pltpu.SemaphoreType.DMA
    yc, vc, lh, ll = pl.pallas_call(
        functools.partial(exchange, nz),
        out_shape=(wide, wide, left, left),
        in_specs=[pl.BlockSpec(memory_space=pl.ANY), vmem, vmem],
        out_specs=(vmem, vmem, vmem, vmem),
        scratch_shapes=[
            pltpu.VMEM((rows, width), F32),
            block, block, block, block, block,
            pltpu.VMEM((2 * size, 2 * size), F32),
            pltpu.VMEM((4 * nz, srows, 2 * size), F32),
            pltpu.VMEM((2 * size, 2 * size), F32),
            dma(()), dma(()), dma((2, 5)), dma((2, nz)), dma((2, 2)), dma((2, 2)),
            dma(()), dma(()), dma(()), dma(()), dma(()), dma(()), dma(()), dma(()),
        ],
        compiler_params=pltpu.CompilerParams(collective_id=0, has_side_effects=True, vmem_limit_bytes=40 << 20),
        name="exchange",
    )(matrix, panels, factors)
    tile = 256 if width % 256 == 0 else width
    return pl.pallas_call(
        apply_update,
        grid=(width // tile,),
        out_shape=jax.ShapeDtypeStruct(matrix.shape, F32),
        in_specs=[
            pl.BlockSpec((rows, tile), lambda i: (0, i)),
            pl.BlockSpec((2, tile, size), lambda i: (0, i, 0)),
            pl.BlockSpec((2, tile, size), lambda i: (0, i, 0)),
            pl.BlockSpec((rows, 4 * size), lambda i: (0, 0)),
            pl.BlockSpec((rows, 4 * size), lambda i: (0, 0)),
        ],
        out_specs=pl.BlockSpec((rows, tile), lambda i: (0, i)),
        name="apply_update",
    )(matrix, yc, vc, lh, ll)


def solution(mesh):
    placed = (P("row", "col"), P(None, "row", None), P())
    return jax.shard_map(
        functools.partial(shards, mesh.shape["col"]),
        mesh=mesh, in_specs=placed, out_specs=P("row", "col"), check_vma=False,
    )
```

time: 775 us -> 104 us (0.13)
  waiting for transfers between devices: 705 us -> 0 us
  Pallas kernels: 0 us -> 96 us
  matrix products: 50.4 us -> 0 us
  between operations: 13.3 us -> 0.02 us
    psum x4 -> x0, waiting for transfers between devices: 609 us -> none  [the longest x2 459 us: row_sums(): lax.psum((transposed_dot(current, vector_rows),) + extra_terms, 'row')]
    pallas_call x0 -> x2, Pallas kernels: none -> 96 us  [the longest x1 87.4 us: shards(): pl.pallas_call(functools.partial(exchange, nz), out_shape=(wide, wide, le...]
    all_gather x1 -> x0, waiting for transfers between devices: 95.2 us -> none  [shards(): gathered = lax.all_gather(panels, 'row', axis=1, tiled=True)]
    dot_general x20 -> x0, matrix products: 50.4 us -> none  [the longest x14 20.8 us: matmul(): return jnp.dot(former, latter, precision=lax.Precision.HIGHEST)]
  transfers between devices with their start and end apart: 5 -> 0, of which waited for: 5 -> 0; matrix products, arithmetic and copies ran while one was open for 3% -> 0% of each run, Pallas kernels for 0% -> 0%
where the time goes in v1:
time: 104 us
  Pallas kernels  96 us (92%)
  local copies, waits for them, and re-layouts  7.82 us (8%)
    pallas_call x1, Pallas kernels, shards(): pl.pallas_call(functools.partial(exchange, nz), out_shape=(wide, wide, le...  87.4 us
    pallas_call x1, Pallas kernels, shards(): pl.pallas_call(apply_update, grid=(width // tile,), out_shape=jax.ShapeDt...  8.58 us
    unnamed x14, local copies, waits for them, and re-layouts  7.82 us

profile of v1, /device:TPU:1, one launch (start us, length us, event | category | flops | bytes accessed | tf_op | source)
XLA Modules:
  0.0 103.9 jit_solution(11710352331791320158)
XLA Ops:
  0.0 0.0 copy-start
  0.0 1.9 %copy-done = f32[448,1792]{1,0:T(8,128)S(1)} copy-done((f32[448,1792]{1,0:T(8,128)S(1)}, f32[448,1792]{1,0:T(8,128)}, u32[]{:S(2)}) %copy-start) | copy-done | bytes 3211288
  1.9 0.0 copy-start.3
  1.9 1.0 copy-done.3
  2.9 0.0 copy-start.6
  2.9 0.9 copy-done.6
  3.8 87.4 %exchange.1 = (f32[2,1792,128]{2,1,0:T(8,128)S(1)}, f32[2,1792,128]{2,1,0:T(8,128)S(1)}, bf16[448,512]{1,0:T(8,128)(2,1)S(1)}, bf16[448,512]{1,0:T(8,128)(2,1)S(1)}) custom-call(f32[448,1792]{1,0:T(8,128)S(1)} %copy-done, f32[2,448,128]{2,1,0:T(8,128)S(1)} %copy-done.3, f32[2,128,128]{2,1,0:T(8,128)S(1)} %copy-done.6), custom_call_target="tpu_custom_call" | custom-call | tf_op jit(solution)/shard_map/exchange/pallas_call | solution.py:263
  91.3 0.0 copy-start.1
  91.3 1.2 %copy-done.1 = f32[2,1792,128]{2,1,0:T(8,128)} copy-done((f32[2,1792,128]{2,1,0:T(8,128)}, f32[2,1792,128]{2,1,0:T(8,128)S(1)}, u32[]{:S(2)}) %copy-start.1) | copy-done | bytes 1835032
  92.5 0.0 copy-start.2
  92.5 1.2 %copy-done.2 = f32[2,1792,128]{2,1,0:T(8,128)} copy-done((f32[2,1792,128]{2,1,0:T(8,128)}, f32[2,1792,128]{2,1,0:T(8,128)S(1)}, u32[]{:S(2)}) %copy-start.2) | copy-done | bytes 1835032
  93.8 0.0 copy-start.4
  93.8 0.8 copy-done.4
  94.5 0.0 copy-start.5
  94.5 0.8 copy-done.5
  95.3 8.6 %apply_update.1 = f32[448,1792]{1,0:T(8,128)} custom-call(f32[448,1792]{1,0:T(8,128)} %a_ref.1, f32[2,1792,128]{2,1,0:T(8,128)} %copy-done.1, f32[2,1792,128]{2,1,0:T(8,128)} %copy-done.2, bf16[448,512]{1,0:T(8,128)(2,1)} %copy-done.4, bf16[448,512]{1,0:T(8,128)(2,1)} %copy-done.5), custom_call_target="tpu_custom_call" | custom-call | tf_op jit(solution)/shard_map/apply_update/pallas_call | solution.py:281
Async XLA Ops:
  0.0 1.9 %copy-start = (f32[448,1792]{1,0:T(8,128)S(1)}, f32[448,1792]{1,0:T(8,128)}, u32[]{:S(2)}) copy-start(f32[448,1792]{1,0:T(8,128)} %a_ref.1) | copy-start | bytes 9633796
  1.9 1.0 copy-start.3
  2.9 0.9 copy-start.6
  91.3 1.2 %copy-start.1 = (f32[2,1792,128]{2,1,0:T(8,128)}, f32[2,1792,128]{2,1,0:T(8,128)S(1)}, u32[]{:S(2)}) copy-start(f32[2,1792,128]{2,1,0:T(8,128)S(1)} %get-tuple-element.9.yc) | copy-start | bytes 5505028
  92.5 1.2 %copy-start.2 = (f32[2,1792,128]{2,1,0:T(8,128)}, f32[2,1792,128]{2,1,0:T(8,128)S(1)}, u32[]{:S(2)}) copy-start(f32[2,1792,128]{2,1,0:T(8,128)S(1)} %get-tuple-element.10.vc) | copy-start | bytes 5505028
  93.8 0.8 copy-start.4
  94.5 0.8 copy-start.5

commit v2 on v1

--- a/solution.py
+++ b/solution.py
@@ -35,10 +35,10 @@
     return one(ah, bh) + (one(ah, bl) + one(al, bh))
 
 
-def exchange(nz, a_hbm, v_ref, f_ref, yc, vc, lh, ll,
-             a_buf, v1, p_buf, rs, y1, yr, sp, srs, sf,
-             a_sem, own_sem, g_send, g1_recv, g2_recv, g3_recv,
-             rs_send, rs_recv, ag_send, ag_recv, ss_send, ss_recv, sg_send, sg_recv):
+def exchange(nz, a_hbm, v_hbm, f_hbm, a_buf, rh, rl, lh, ll,
+             ah, al, v_ref, f_ref, vc, yc, v1, p_buf, rs, y1, yr, sp, srs, szs, sf,
+             a_sem, v_sem, f_sem, own_sem, g_send, g1_recv, g2_recv, g3_recv,
+             rs_send, rs_recv, ag_send, ag_recv, ss_send, ss_recv, sg_send, sg_recv, sz_send, sz_recv):
     row, col = lax.axis_index("row"), lax.axis_index("col")
     z, quad = row // 4, row % 4
     yl, core = quad // 2, quad % 2
@@ -60,11 +60,13 @@
     def drain(ref, sem):
         pltpu.make_async_copy(ref, ref, sem).wait()
 
+    load_v = pltpu.make_async_copy(v_hbm, v_ref, v_sem)
+    load_v.start()
+    load_f = pltpu.make_async_copy(f_hbm, f_ref, f_sem)
+    load_f.start()
     load = pltpu.make_async_copy(a_hbm, a_buf, a_sem)
     load.start()
     own = pltpu.make_async_copy(at(v_ref, col, piece), at(v1, z, piece), own_sem)
-    own.start()
-
     def zpeer(step):
         return (z + step) % nz
 
@@ -84,43 +86,46 @@
 
     lax.fori_loop(1, nz, greet_z, 0)
     lax.fori_loop(1, plane, greet_plane, 0)
+    load_v.wait()
+    own.start()
+    own.wait()
     pl.semaphore_wait(barrier, nz - 1 + plane - 1)
 
-    def zorder(index):
-        return (z + ((index % 2) * 2 - 1) * ((index + 1) // 2) + nz) % nz
+    turn = col + 2 * quad
+
+    def hop(index):
+        return 1 + (index + turn) % (nz - 1)
 
     def spread(src, dst, which):
         def body(index, carry):
-            to = zorder(nz - 1 - index)
+            to = (z + hop(index)) % nz
             send(src, at(dst, z, piece), g_send.at[which, 0], g1_recv.at[which, z], to * 4 + quad, col)
             return carry
 
         lax.fori_loop(0, nz - 1, body, 0)
 
-    def deliver(held, full, which):
+    def hand_on(held, full, which, target):
+        src = at(held, target, piece)
+        dst = full.at[:, pl.ds(pl.multiple_of(quad * rows + col * piece, 8), piece), :]
+
+        send(src, dst, g_send.at[which, 1], g2_recv.at[which, yl], z * 4 + (1 - yl) * 2 + core, target)
+
+        @pl.when(target != col)
+        def _():
+            send(src, dst, g_send.at[which, 2], g2_recv.at[which, yl], row, target)
+
+        @pl.when(target == col)
+        def _():
+            pltpu.make_async_copy(src, dst, g2_recv.at[which, yl]).start()
+
+    def deliver(held, full, which, first, last):
         def body(index, carry):
-            target = zorder(index)
-            src = at(held, target, piece)
-
-            @pl.when(index > 0)
-            def _():
-                drain(src, g1_recv.at[which, target])
-
-            dst = full.at[:, pl.ds(pl.multiple_of(quad * rows + col * piece, 8), piece), :]
-
-            send(src, dst, g_send.at[which, 1], g2_recv.at[which, yl], z * 4 + (1 - yl) * 2 + core, target)
-
-            @pl.when(target != col)
-            def _():
-                send(src, dst, g_send.at[which, 2], g2_recv.at[which, yl], row, target)
-
-            @pl.when(target == col)
-            def _():
-                pltpu.make_async_copy(src, dst, g2_recv.at[which, yl]).start()
-
+            target = (z + nz - hop(index)) % nz
+            drain(at(held, target, piece), g1_recv.at[which, target])
+            hand_on(held, full, which, target)
             return carry
 
-        lax.fori_loop(0, nz, body, 0)
+        lax.fori_loop(first, last, body, 0)
 
     def relay(full, which):
         for side in range(2):
@@ -138,22 +143,32 @@
         for side in range(2):
             drain(at(full, 0, rows), g_send.at[which, 3 + side])
 
-    own.wait()
+    half = v_ref.shape[2]
+
+    def split_into(full, base):
+        for panel in range(2):
+            high, low = halves(full[panel])
+            rh[:, base + panel * half:base + (panel + 1) * half] = high
+            rl[:, base + panel * half:base + (panel + 1) * half] = low
+
     spread(at(v1, z, piece), v1, 0)
-    deliver(v1, vc, 0)
+    hand_on(v1, vc, 0, z)
+    load.wait()
+    ah[...], al[...] = halves(a_buf[...])
+    deliver(v1, vc, 0, 0, nz - 1)
     relay(vc, 0)
-    load.wait()
 
     for side in range(2):
         partner(vc, 0, side)
         span = slice(side * 2 * rows, (side + 1) * 2 * rows)
-        left = halves(a_buf[:, span])
         for panel in range(2):
-            part = dot3(left, halves(vc[panel, span, :]))
-            if side == 0:
-                p_buf[panel] = part
-            else:
-                p_buf[panel] = p_buf[panel] + part
+            high, low = halves(vc[panel, span, :])
+            rh[span, (2 + panel) * half:(3 + panel) * half] = high
+            rl[span, (2 + panel) * half:(3 + panel) * half] = low
+        part = dot3((ah[:, span], al[:, span]), (rh[span, 2 * half:], rl[span, 2 * half:]))
+        for panel in range(2):
+            one = part[:, panel * half:(panel + 1) * half]
+            p_buf[panel] = one if side == 0 else p_buf[panel] + one
 
     def scatter(step, carry):
         to = (col + step) % nz
@@ -173,19 +188,13 @@
 
     spread(at(y1, z, piece), y1, 1)
 
-    def gather(step, carry):
-        to = (col + step) % nz
-        send(at(yr, col, piece), at(yr, col, piece), ag_send, ag_recv, row, to)
-        return carry
-
-    lax.fori_loop(1, nz, gather, 0)
-    deliver(y1, yc, 1)
-
-    half = sp.shape[0] // 2
-    sp[:half, :half] = exact(v1[0], y1[0], TN)
-    sp[:half, half:] = exact(v1[0], y1[1], TN)
-    sp[half:, :half] = exact(v1[0], v1[1], TN)
-    sp[half:, half:] = exact(v1[1], y1[1], TN)
+    hand_on(y1, yc, 1, z)
+
+    va, vb = v_ref[0, mine_rows, :], v_ref[1, mine_rows, :]
+    sp[:half, :half] = exact(va, total[0], TN)
+    sp[:half, half:] = exact(va, total[1], TN)
+    sp[half:, :half] = exact(va, vb, TN)
+    sp[half:, half:] = exact(vb, total[1], TN)
 
     def split_sum(step, carry):
         to_row, to_col = ppeer(step)
@@ -196,9 +205,26 @@
     lax.fori_loop(1, plane, split_sum, 0)
     s_rows = pl.ds(pl.multiple_of(mine * srows, 8), srows)
     srs[mine] = sp[s_rows, :]
-    relay(yc, 1)
+
+    def gather(step, carry):
+        to = (col + step) % nz
+        send(at(yr, col, piece), at(yr, col, piece), ag_send, ag_recv, row, to)
+        return carry
+
+    lax.fori_loop(1, nz, gather, 0)
+    cuts = (nz - 1) // 3, 2 * (nz - 1) // 3
+    deliver(y1, yc, 1, 0, cuts[0])
     drain(srs.at[0:plane - 1], ss_recv)
-    sf[s_rows, :] = jnp.sum(srs[...], axis=0)
+    szs[z] = jnp.sum(srs[...], axis=0)
+
+    def level(step, carry):
+        send(szs.at[z], szs.at[z], sz_send, sz_recv, zpeer(step) * 4 + quad, col)
+        return carry
+
+    lax.fori_loop(1, nz, level, 0)
+    deliver(y1, yc, 1, cuts[0], cuts[1])
+    drain(szs.at[0:nz - 1], sz_recv)
+    sf[s_rows, :] = jnp.sum(szs[...], axis=0)
 
     def join_sum(step, carry):
         to_row, to_col = ppeer(step)
@@ -207,9 +233,12 @@
         return carry
 
     lax.fori_loop(1, plane, join_sum, 0)
+    deliver(y1, yc, 1, cuts[1], nz - 1)
+    relay(yc, 1)
     drain(at(yr, 0, (nz - 1) * piece), ag_recv)
     drain(sf.at[0:(plane - 1) * srows, :], sg_recv)
 
+    load_f.wait()
     f1, f2 = f_ref[0], f_ref[1]
     s11, s12 = sf[:half, :half], sf[:half, half:]
     gram, s22 = sf[half:, :half], sf[half:, half:]
@@ -237,61 +266,78 @@
 
     for side in range(2):
         partner(yc, 1, side)
+    split_into(yc, 0)
     settle(v1, vc, 0)
     settle(y1, yc, 1)
     drain(at(rs, 0, (nz - 1) * piece), rs_send)
     drain(at(rs, 0, (nz - 1) * piece), ag_send)
     drain(srs.at[0:plane - 1], ss_send)
     drain(srs.at[0:plane - 1], sg_send)
-
-
-def apply_update(a_ref, yc, vc, lh, ll, out):
-    right = jnp.concatenate([yc[0], yc[1], vc[0], vc[1]], axis=1)
-    out[...] = a_ref[...] - dot3((lh[...], ll[...]), halves(right), NT)
+    drain(szs.at[0:nz - 1], sz_send)
+
+
+def apply_update(tile, a_ref, rh, rl, lh, ll, out, stage, sems):
+    count = out.shape[1] // tile
+
+    def store(slot, index):
+        span = pl.ds(pl.multiple_of(index * tile, tile), tile)
+        return pltpu.make_async_copy(stage.at[slot], out.at[:, span], sems.at[slot])
+
+    def body(index, carry):
+        slot = index % 2
+
+        @pl.when(index >= 2)
+        def _():
+            store(slot, index - 2).wait()
+
+        span = pl.ds(pl.multiple_of(index * tile, tile), tile)
+        stage[slot] = a_ref[:, span] - dot3((lh[...], ll[...]), (rh[span, :], rl[span, :]), NT)
+        store(slot, index).start()
+        return carry
+
+    lax.fori_loop(0, count, body, 0)
+    for index in range(max(count - 2, 0), count):
+        store(index % 2, index).wait()
 
 
 def shards(nz, matrix, panels, factors):
     rows, width = matrix.shape
     size = panels.shape[2]
-    piece = rows // nz
     srows = 2 * size // (4 * nz)
     vmem = pl.BlockSpec(memory_space=pltpu.VMEM)
-    wide = jax.ShapeDtypeStruct((2, width, size), F32)
+    hbm = pl.BlockSpec(memory_space=pltpu.HBM)
+    right = jax.ShapeDtypeStruct((width, 4 * size), BF16)
     left = jax.ShapeDtypeStruct((rows, 4 * size), BF16)
     block = pltpu.VMEM((2, rows, size), F32)
+    wide = pltpu.VMEM((2, width, size), F32)
+    square = pltpu.VMEM((2 * size, 2 * size), F32)
     dma = pltpu.SemaphoreType.DMA
-    yc, vc, lh, ll = pl.pallas_call(
+    held = pl.pallas_call(
         functools.partial(exchange, nz),
-        out_shape=(wide, wide, left, left),
-        in_specs=[pl.BlockSpec(memory_space=pl.ANY), vmem, vmem],
-        out_specs=(vmem, vmem, vmem, vmem),
+        out_shape=(jax.ShapeDtypeStruct(matrix.shape, F32), right, right, left, left),
+        in_specs=[hbm, hbm, hbm],
+        out_specs=(vmem,) * 5,
         scratch_shapes=[
-            pltpu.VMEM((rows, width), F32),
+            pltpu.VMEM((rows, width), BF16), pltpu.VMEM((rows, width), BF16),
+            block, pltpu.VMEM(factors.shape, F32), wide, wide,
             block, block, block, block, block,
-            pltpu.VMEM((2 * size, 2 * size), F32),
-            pltpu.VMEM((4 * nz, srows, 2 * size), F32),
-            pltpu.VMEM((2 * size, 2 * size), F32),
-            dma(()), dma(()), dma((2, 5)), dma((2, nz)), dma((2, 2)), dma((2, 2)),
-            dma(()), dma(()), dma(()), dma(()), dma(()), dma(()), dma(()), dma(()),
-        ],
+            square, pltpu.VMEM((4 * nz, srows, 2 * size), F32),
+            pltpu.VMEM((nz, srows, 2 * size), F32), square,
+            dma(()), dma(()), dma(()), dma(()), dma((2, 5)), dma((2, nz)), dma((2, 2)), dma((2, 2)),
+        ] + [dma(())] * 10,
         compiler_params=pltpu.CompilerParams(collective_id=0, has_side_effects=True, vmem_limit_bytes=40 << 20),
         name="exchange",
     )(matrix, panels, factors)
     tile = 256 if width % 256 == 0 else width
     return pl.pallas_call(
-        apply_update,
-        grid=(width // tile,),
+        functools.partial(apply_update, tile),
         out_shape=jax.ShapeDtypeStruct(matrix.shape, F32),
-        in_specs=[
-            pl.BlockSpec((rows, tile), lambda i: (0, i)),
-            pl.BlockSpec((2, tile, size), lambda i: (0, i, 0)),
-            pl.BlockSpec((2, tile, size), lambda i: (0, i, 0)),
-            pl.BlockSpec((rows, 4 * size), lambda i: (0, 0)),
-            pl.BlockSpec((rows, 4 * size), lambda i: (0, 0)),
-        ],
-        out_specs=pl.BlockSpec((rows, tile), lambda i: (0, i)),
+        in_specs=[vmem] * 5,
+        out_specs=hbm,
+        scratch_shapes=[pltpu.VMEM((2, rows, tile), F32), dma((2,))],
+        compiler_params=pltpu.CompilerParams(vmem_limit_bytes=24 << 20),
         name="apply_update",
-    )(matrix, yc, vc, lh, ll)
+    )(*held)
 
 
 def solution(mesh):

time: 104 us -> 91.5 us (0.88)
  the two profiles are of different devices: /device:TPU:1 before, /device:TPU:2 now
where the time goes in v2:
time: 91.5 us; the launch traced here: 91.3 us
  Pallas kernels  87.4 us (96%)
  local copies, waits for them, and re-layouts  3.83 us (4%)
    pallas_call x1, Pallas kernels, shards(): pl.pallas_call(functools.partial(exchange, nz), out_shape=(jax.ShapeDtype...  82.1 us
    pallas_call x1, Pallas kernels, shards(): pl.pallas_call(functools.partial(apply_update, tile), out_shape=jax.Shape...  5.31 us
    unnamed x6, local copies, waits for them, and re-layouts  3.83 us

profile of v2, /device:TPU:2, one launch (start us, length us, event | category | flops | bytes accessed | tf_op | source)
XLA Modules:
  0.0 91.3 jit_solution(7063452151306742637)
XLA Ops:
  0.0 0.0 copy-start
  0.0 1.9 %copy-done = f32[448,1792]{1,0:T(8,128)S(1)} copy-done((f32[448,1792]{1,0:T(8,128)S(1)}, f32[448,1792]{1,0:T(8,128)}, u32[]{:S(2)}) %copy-start) | copy-done | bytes 3211288
  1.9 0.0 copy-start.1
  1.9 1.0 %copy-done.1 = f32[2,448,128]{2,1,0:T(8,128)S(1)} copy-done((f32[2,448,128]{2,1,0:T(8,128)S(1)}, f32[2,448,128]{2,1,0:T(8,128)}, u32[]{:S(2)}) %copy-start.1) | copy-done | bytes 458776
  2.9 0.0 copy-start.2
  2.9 0.9 copy-done.2
  3.8 82.1 %exchange.1 = (f32[448,1792]{1,0:T(8,128)S(1)}, bf16[1792,512]{1,0:T(8,128)(2,1)S(1)}, bf16[1792,512]{1,0:T(8,128)(2,1)S(1)}, bf16[448,512]{1,0:T(8,128)(2,1)S(1)}, bf16[448,512]{1,0:T(8,128)(2,1)S(1)}) custom-call(f32[448,1792]{1,0:T(8,128)S(1)} %copy-done, f32[2,448,128]{2,1,0:T(8,128)S(1)} %copy-done.1, f32[2,128,128]{2,1,0:T(8,128)S(1)} %copy-done.2), custom_call_target="tpu_custom_call" | custom-call | tf_op jit(solution)/shard_map/exchange/pallas_call | solution.py:315
  86.0 5.3 %apply_update.1 = f32[448,1792]{1,0:T(8,128)} custom-call(f32[448,1792]{1,0:T(8,128)S(1)} %get-tuple-element.10.a_ref, bf16[1792,512]{1,0:T(8,128)(2,1)S(1)} %get-tuple-element.11.rh, bf16[1792,512]{1,0:T(8,128)(2,1)S(1)} %get-tuple-element.12.rl, bf16[448,512]{1,0:T(8,128)(2,1)S(1)} %get-tuple-element.13.lh, bf16[448,512]{1,0:T(8,128)(2,1)S(1)} %get-tuple-element.14.ll), custom_call_target="tpu_custom_call" | custom-call | tf_op jit(solution)/shard_map/apply_update/pallas_call | solution.py:332
Async XLA Ops:
  0.0 1.9 %copy-start = (f32[448,1792]{1,0:T(8,128)S(1)}, f32[448,1792]{1,0:T(8,128)}, u32[]{:S(2)}) copy-start(f32[448,1792]{1,0:T(8,128)} %a_hbm.1) | copy-start | bytes 9633796
  1.9 1.0 %copy-start.1 = (f32[2,448,128]{2,1,0:T(8,128)S(1)}, f32[2,448,128]{2,1,0:T(8,128)}, u32[]{:S(2)}) copy-start(f32[2,448,128]{2,1,0:T(8,128)} %v_hbm.1) | copy-start | bytes 1376260
  2.9 0.9 copy-start.2

commit v3 on v2

v3 whole, which is shorter than its diff:
```python
import functools

import jax
import jax.numpy as jnp
from jax import lax
from jax.experimental import pallas as pl
from jax.experimental.pallas import tpu as pltpu
from jax.sharding import PartitionSpec as P

MESH = pl.DeviceIdType.MESH
F32 = jnp.float32
BF16 = jnp.bfloat16
NN = (((1,), (0,)), ((), ()))
NT = (((1,), (1,)), ((), ()))
TN = (((0,), (0,)), ((), ()))


def exact(a, b, dims=NN):
    return lax.dot_general(
        a, b, dims, precision=lax.Precision.HIGHEST, preferred_element_type=F32
    )


def halves(value):
    high = value.astype(BF16)
    return high, (value - high.astype(F32)).astype(BF16)


def exchange(nz, a_hbm, v_hbm, f_hbm, a_buf, right, lh, ll,
             ah, al, v_ref, f_ref, vc, yc, v1, p_buf, rs, y1, yr, sp, srs, szs, sf,
             a_sem, v_sem, f_sem, own_sem, g_send, g1_recv, g2_recv, g3_recv,
             rs_send, rs_recv, ag_send, ag_recv, ss_send, ss_recv, sg_send, sg_recv, sz_send, sz_recv):
    row, col = lax.axis_index("row"), lax.axis_index("col")
    z, quad = row // 4, row % 4
    yl, core = quad // 2, quad % 2
    rows, width = a_buf.shape
    size = v_ref.shape[2]
    piece = rows // nz
    plane = 4 * nz
    srows = sp.shape[1] // plane
    mine = col * 4 + quad

    def block(index, step):
        return pl.ds(pl.multiple_of(index * step, 8), step)

    def send(src, dst, ssem, rsem, to_row, to_col):
        pltpu.make_async_remote_copy(
            src_ref=src, dst_ref=dst, send_sem=ssem, recv_sem=rsem,
            device_id=(to_row, to_col), device_id_type=MESH,
        ).start()

    def drain(ref, sem):
        pltpu.make_async_copy(ref, ref, sem).wait()

    load_v = pltpu.make_async_copy(v_hbm, v_ref, v_sem)
    load_v.start()
    load_f = pltpu.make_async_copy(f_hbm, f_ref, f_sem)
    load_f.start()
    load = pltpu.make_async_copy(a_hbm, a_buf, a_sem)
    load.start()
    mine_rows, z_rows, s_rows = block(col, piece), block(z, piece), block(mine, srows)
    own = pltpu.make_async_copy(v_ref.at[:, mine_rows, :], v1.at[:, z_rows, :], own_sem)

    def zpeer(step):
        return (z + step) % nz

    def ppeer(step):
        other = (mine + step) % plane
        return z * 4 + other % 4, other // 4

    barrier = pltpu.get_barrier_semaphore()

    def greet_z(step, carry):
        pl.semaphore_signal(barrier, inc=1, device_id=(zpeer(step) * 4 + quad, col), device_id_type=MESH)
        return carry

    def greet_plane(step, carry):
        pl.semaphore_signal(barrier, inc=1, device_id=ppeer(step), device_id_type=MESH)
        return carry

    lax.fori_loop(1, nz, greet_z, 0)
    lax.fori_loop(1, plane, greet_plane, 0)
    load_v.wait()
    own.start()
    own.wait()
    pl.semaphore_wait(barrier, nz - 1 + plane - 1)

    turn = col + 2 * quad

    def hop(index):
        return (index + turn) % nz

    def spread(held, which):
        part = held.at[z_rows, :]

        def body(index, carry):
            to = (z + hop(index)) % nz

            @pl.when(to != z)
            def _():
                send(part, part, g_send.at[which, 0], g1_recv.at[which, z], to * 4 + quad, col)

            return carry

        lax.fori_loop(0, nz, body, 0)

    def hand_on(held, full, which, target):
        src = held.at[block(target, piece), :]
        dst = full.at[pl.ds(pl.multiple_of(quad * rows + col * piece, 8), piece), :]
        send(src, dst, g_send.at[which, 1], g2_recv.at[which, yl], z * 4 + (1 - yl) * 2 + core, target)

        @pl.when(target != col)
        def _():
            send(src, dst, g_send.at[which, 2], g2_recv.at[which, yl], row, target)

        @pl.when(target == col)
        def _():
            pltpu.make_async_copy(src, dst, g2_recv.at[which, yl]).start()

    def deliver(held, full, which, first, last):
        def body(index, carry):
            target = (z + nz - hop(index)) % nz

            @pl.when(target != z)
            def _():
                drain(held.at[block(target, piece), :], g1_recv.at[which, target])

            hand_on(held, full, which, target)
            return carry

        lax.fori_loop(first, last, body, 0)

    def relay(full, which):
        for side in range(2):
            part = full.at[block(side * 2 + core, rows), :]
            drain(part, g2_recv.at[which, side])
            send(part, part, g_send.at[which, 3 + side], g3_recv.at[which, side], z * 4 + yl * 2 + (1 - core), col)

    def partner(full, which, side):
        drain(full.at[block(side * 2 + (1 - core), rows), :], g3_recv.at[which, side])

    def settle(held, full, which):
        drain(held.at[0:(nz - 1) * piece, :], g_send.at[which, 0])
        drain(held.at[0:nz * piece, :], g_send.at[which, 1])
        drain(held.at[0:(nz - 1) * piece, :], g_send.at[which, 2])
        for side in range(2):
            drain(full.at[0:rows, :], g_send.at[which, 3 + side])

    def sum_start(group):
        def body(step, carry):
            to_row, to_col = ppeer(step)
            other = (mine + step) % plane
            send(sp.at[group, block(other, srows), :], srs.at[group, mine], ss_send.at[group], ss_recv.at[group], to_row, to_col)
            return carry

        lax.fori_loop(1, plane, body, 0)
        srs[group, mine] = sp[group, s_rows, :]

    def sum_level(group):
        drain(srs.at[group, 0:plane - 1], ss_recv.at[group])
        szs[group, z] = jnp.sum(srs[group], axis=0)

        def body(step, carry):
            part = szs.at[group, z]
            send(part, part, sz_send.at[group], sz_recv.at[group], zpeer(step) * 4 + quad, col)
            return carry

        lax.fori_loop(1, nz, body, 0)

    def sum_share(group):
        drain(szs.at[group, 0:nz - 1], sz_recv.at[group])
        sf[group, s_rows, :] = jnp.sum(szs[group], axis=0)

        def body(step, carry):
            to_row, to_col = ppeer(step)
            part = sf.at[group, s_rows, :]
            send(part, part, sg_send.at[group], sg_recv.at[group], to_row, to_col)
            return carry

        lax.fori_loop(1, plane, body, 0)

    def sum_end(group):
        drain(sf.at[group, 0:(plane - 1) * srows, :], sg_recv.at[group])

    def sum_settle(group):
        drain(srs.at[group, 0:plane - 1], ss_send.at[group])
        drain(szs.at[group, 0:nz - 1], sz_send.at[group])
        drain(srs.at[group, 0:plane - 1], sg_send.at[group])

    for panel in range(2):
        spread(v1.at[panel], panel)
    va, vb = v_ref[0, mine_rows, :], v_ref[1, mine_rows, :]
    sp[0, :size] = exact(va, vb, TN)
    sp[0, size:] = sp[0, :size]
    sum_start(0)
    load.wait()
    ah[...], al[...] = halves(a_buf[...])
    deliver(v1.at[0], vc.at[0], 0, 0, nz)
    deliver(v1.at[1], vc.at[1], 1, 0, nz)
    sum_level(0)

    def fold(full, slot, span):
        high, low = halves(full[span, :])
        right[span, 2 * slot * size:(2 * slot + 1) * size] = high
        right[span, (2 * slot + 1) * size:(2 * slot + 2) * size] = low

    for panel in range(2):
        relay(vc.at[panel], panel)
        slot = 2 + panel
        base = 2 * slot * size
        for side in range(2):
            partner(vc.at[panel], panel, side)
            span = slice(side * 2 * rows, (side + 1) * 2 * rows)
            fold(vc.at[panel], slot, span)
            both = lax.dot_general(ah[:, span], right[span, base:base + 2 * size], NN, preferred_element_type=F32)
            part = lax.dot_general(al[:, span], right[span, base:base + size], NN, preferred_element_type=F32)
            part = part + both[:, size:] + both[:, :size]
            p_buf[panel] = part if side == 0 else p_buf[panel] + part

        def scatter(step, carry, panel=panel):
            to = (col + step) % nz
            send(p_buf.at[panel, block(to, piece), :], rs.at[panel, mine_rows, :], rs_send.at[panel], rs_recv.at[panel], row, to)
            return carry

        lax.fori_loop(1, nz, scatter, 0)
        rs[panel, mine_rows, :] = p_buf[panel, mine_rows, :]
    sum_share(0)

    for panel in range(2):
        drain(rs.at[panel, 0:(nz - 1) * piece, :], rs_recv.at[panel])
        total = rs[panel, 0:piece, :]
        for other in range(1, nz):
            total = total + rs[panel, other * piece:(other + 1) * piece, :]
        y1[panel, z_rows, :] = total
        yr[panel, mine_rows, :] = total
        spread(y1.at[panel], 2 + panel)
        sp[1 + panel, :size] = exact(vb if panel else va, total, TN)
        sp[1 + panel, size:] = exact(vb, total, TN)
        sum_start(1 + panel)

    def gather_all(panel):
        def body(step, carry):
            to = (col + step) % nz
            part = yr.at[panel, mine_rows, :]
            send(part, part, ag_send.at[panel], ag_recv.at[panel], row, to)
            return carry

        lax.fori_loop(1, nz, body, 0)

    deliver(y1.at[0], yc.at[0], 2, 0, nz)
    sum_level(1)
    gather_all(0)
    deliver(y1.at[1], yc.at[1], 3, 0, nz)
    sum_level(2)
    gather_all(1)
    sum_share(1)
    relay(yc.at[0], 2)
    sum_share(2)

    load_f.wait()
    f1, f2 = f_ref[0], f_ref[1]
    va, vb = v_ref[0], v_ref[1]
    sum_end(0)
    gram = sf[0, :size]
    gf = exact(gram, f2)
    e = exact(f1, gf)
    lefts = [exact(va, f1, NT) - exact(vb, e, NT), exact(vb, f2, NT)]
    for panel in range(2):
        drain(yr.at[panel, 0:(nz - 1) * piece, :], ag_recv.at[panel])
    ya, yb = yr[0], yr[1]
    sum_end(1)
    s11, s21 = sf[1, :size], sf[1, size:]
    k1 = exact(exact(f1, s11, TN), f1)
    fs = exact(f1, s21, (((0,), (1,)), ((), ())))
    kg = exact(k1, gram)
    mixed = exact(kg - fs, f2)
    gt = exact(gram, fs - 0.5 * kg, TN)
    lefts.append(exact(ya, f1) - exact(va, k1) + exact(vb, mixed, NT))
    rest = exact(yb, f2) - exact(ya, e) + exact(va, mixed)
    for panel in range(2):
        if panel:
            relay(yc.at[1], 3)
        for side in range(2):
            partner(yc.at[panel], 2 + panel, side)
        fold(yc.at[panel], panel, slice(0, width))
    sum_end(2)
    k2 = exact(exact(f2, sf[2, :size] - gt - gt.T, TN), f2)
    lefts.append(rest - exact(vb, k2))
    for index, part in enumerate(lefts):
        high, low = halves(part)
        lh[:, 2 * index * size:(2 * index + 1) * size] = high
        lh[:, (2 * index + 1) * size:(2 * index + 2) * size] = high
        ll[:, index * size:(index + 1) * size] = low

    for panel in range(2):
        settle(v1.at[panel], vc.at[panel], panel)
        settle(y1.at[panel], yc.at[panel], 2 + panel)
        drain(rs.at[panel, 0:(nz - 1) * piece, :], rs_send.at[panel])
        drain(rs.at[panel, 0:(nz - 1) * piece, :], ag_send.at[panel])
    for group in range(3):
        sum_settle(group)


def apply_update(tile, size, a_ref, right, lh, ll, out, stage, sems):
    count = out.shape[1] // tile

    def store(slot, index):
        span = pl.ds(pl.multiple_of(index * tile, tile), tile)
        return pltpu.make_async_copy(stage.at[slot], out.at[:, span], sems.at[slot])

    def body(index, carry):
        slot = index % 2

        @pl.when(index >= 2)
        def _():
            store(slot, index - 2).wait()

        span = pl.ds(pl.multiple_of(index * tile, tile), tile)
        highs = jnp.concatenate([right[span, 2 * s * size:(2 * s + 1) * size] for s in range(4)], axis=1)
        drop = lax.dot_general(ll[...], highs, NT, preferred_element_type=F32)
        drop = drop + lax.dot_general(lh[...], right[span, :], NT, preferred_element_type=F32)
        stage[slot] = a_ref[:, span] - drop
        store(slot, index).start()
        return carry

    lax.fori_loop(0, count, body, 0)
    for index in range(max(count - 2, 0), count):
        store(index % 2, index).wait()


def shards(nz, matrix, panels, factors):
    rows, width = matrix.shape
    size = panels.shape[2]
    srows = 2 * size // (4 * nz)
    vmem = pl.BlockSpec(memory_space=pltpu.VMEM)
    hbm = pl.BlockSpec(memory_space=pltpu.HBM)
    block = pltpu.VMEM((2, rows, size), F32)
    wide = pltpu.VMEM((2, width, size), F32)
    sums = pltpu.VMEM((3, 2 * size, size), F32)
    dma = pltpu.SemaphoreType.DMA
    held = pl.pallas_call(
        functools.partial(exchange, nz),
        out_shape=(
            jax.ShapeDtypeStruct(matrix.shape, F32),
            jax.ShapeDtypeStruct((width, 8 * size), BF16),
            jax.ShapeDtypeStruct((rows, 8 * size), BF16),
            jax.ShapeDtypeStruct((rows, 4 * size), BF16),
        ),
        in_specs=[hbm, hbm, hbm],
        out_specs=(vmem,) * 4,
        scratch_shapes=[
            pltpu.VMEM((rows, width), BF16), pltpu.VMEM((rows, width), BF16),
            block, pltpu.VMEM(factors.shape, F32), wide, wide,
            block, block, block, block, block,
            sums, pltpu.VMEM((3, 4 * nz, srows, size), F32),
            pltpu.VMEM((3, nz, srows, size), F32), sums,
            dma(()), dma(()), dma(()), dma(()), dma((4, 5)), dma((4, nz)), dma((4, 2)), dma((4, 2)),
        ] + [dma((2,))] * 4 + [dma((3,))] * 6,
        compiler_params=pltpu.CompilerParams(collective_id=0, has_side_effects=True, vmem_limit_bytes=40 << 20),
        name="exchange",
    )(matrix, panels, factors)
    tile = 256 if width % 256 == 0 else width
    return pl.pallas_call(
        functools.partial(apply_update, tile, size),
        out_shape=jax.ShapeDtypeStruct(matrix.shape, F32),
        in_specs=[vmem] * 4,
        out_specs=hbm,
        scratch_shapes=[pltpu.VMEM((2, rows, tile), F32), dma((2,))],
        compiler_params=pltpu.CompilerParams(vmem_limit_bytes=24 << 20),
        name="apply_update",
    )(*held)


def solution(mesh):
    placed = (P("row", "col"), P(None, "row", None), P())
    return jax.shard_map(
        functools.partial(shards, mesh.shape["col"]),
        mesh=mesh, in_specs=placed, out_specs=P("row", "col"), check_vma=False,
    )
```

time: 91.5 us -> 78.3 us (0.86)
  the two profiles are of different devices: /device:TPU:2 before, /device:TPU:1 now
where the time goes in v3:
time: 78.3 us; the launch traced here: 78.1 us
  Pallas kernels  74.3 us (95%)
  local copies, waits for them, and re-layouts  3.83 us (5%)
    pallas_call x1, Pallas kernels, shards(): pl.pallas_call(functools.partial(exchange, nz), out_shape=(jax.ShapeDtype...  68.9 us
    pallas_call x1, Pallas kernels, shards(): pl.pallas_call(functools.partial(apply_update, tile, size), out_shape=jax...  5.33 us
    unnamed x6, local copies, waits for them, and re-layouts  3.83 us

profile of v3, /device:TPU:1, one launch (start us, length us, event | category | flops | bytes accessed | tf_op | source)
XLA Modules:
  0.0 78.1 jit_solution(6341080820334656278)
XLA Ops:
  0.0 0.0 copy-start
  0.0 1.9 %copy-done = f32[448,1792]{1,0:T(8,128)S(1)} copy-done((f32[448,1792]{1,0:T(8,128)S(1)}, f32[448,1792]{1,0:T(8,128)}, u32[]{:S(2)}) %copy-start) | copy-done | bytes 3211288
  1.9 0.0 copy-start.1
  1.9 1.0 %copy-done.1 = f32[2,448,128]{2,1,0:T(8,128)S(1)} copy-done((f32[2,448,128]{2,1,0:T(8,128)S(1)}, f32[2,448,128]{2,1,0:T(8,128)}, u32[]{:S(2)}) %copy-start.1) | copy-done | bytes 458776
  2.9 0.0 copy-start.2
  2.9 0.9 %copy-done.2 = f32[2,128,128]{2,1,0:T(8,128)S(1)} copy-done((f32[2,128,128]{2,1,0:T(8,128)S(1)}, f32[2,128,128]{2,1,0:T(8,128)}, u32[]{:S(2)}) %copy-start.2) | copy-done | bytes 131096
  3.8 68.9 %exchange.1 = (f32[448,1792]{1,0:T(8,128)S(1)}, bf16[1792,1024]{1,0:T(8,128)(2,1)S(1)}, bf16[448,1024]{1,0:T(8,128)(2,1)S(1)}, bf16[448,512]{1,0:T(8,128)(2,1)S(1)}) custom-call(f32[448,1792]{1,0:T(8,128)S(1)} %copy-done, f32[2,448,128]{2,1,0:T(8,128)S(1)} %copy-done.1, f32[2,128,128]{2,1,0:T(8,128)S(1)} %copy-done.2), custom_call_target="tpu_custom_call" | custom-call | tf_op jit(solution)/shard_map/exchange/pallas_call | solution.py:341
  72.8 5.3 %apply_update.1 = f32[448,1792]{1,0:T(8,128)} custom-call(f32[448,1792]{1,0:T(8,128)S(1)} %get-tuple-element.9.a_ref, bf16[1792,1024]{1,0:T(8,128)(2,1)S(1)} %get-tuple-element.10.right, bf16[448,1024]{1,0:T(8,128)(2,1)S(1)} %get-tuple-element.11.lh, bf16[448,512]{1,0:T(8,128)(2,1)S(1)} %get-tuple-element.12.ll), custom_call_target="tpu_custom_call" | custom-call | tf_op jit(solution)/shard_map/apply_update/pallas_call | solution.py:363
Async XLA Ops:
  0.0 1.9 %copy-start = (f32[448,1792]{1,0:T(8,128)S(1)}, f32[448,1792]{1,0:T(8,128)}, u32[]{:S(2)}) copy-start(f32[448,1792]{1,0:T(8,128)} %a_hbm.1) | copy-start | bytes 9633796
  1.9 1.0 %copy-start.1 = (f32[2,448,128]{2,1,0:T(8,128)S(1)}, f32[2,448,128]{2,1,0:T(8,128)}, u32[]{:S(2)}) copy-start(f32[2,448,128]{2,1,0:T(8,128)} %v_hbm.1) | copy-start | bytes 1376260
  2.9 0.9 %copy-start.2 = (f32[2,128,128]{2,1,0:T(8,128)S(1)}, f32[2,128,128]{2,1,0:T(8,128)}, u32[]{:S(2)}) copy-start(f32[2,128,128]{2,1,0:T(8,128)} %f_hbm.1) | copy-start | bytes 393220

commit v4 on v3

--- a/solution.py
+++ b/solution.py
@@ -26,10 +26,17 @@
     return high, (value - high.astype(F32)).astype(BF16)
 
 
-def exchange(nz, a_hbm, v_hbm, f_hbm, a_buf, right, lh, ll,
-             ah, al, v_ref, f_ref, vc, yc, v1, p_buf, rs, y1, yr, sp, srs, szs, sf,
+def drop(left, low, right, span):
+    size = right.shape[1] // 4
+    highs = jnp.concatenate([right[span, 0:size], right[span, 2 * size:3 * size]], axis=1)
+    value = lax.dot_general(low[...], highs, NT, preferred_element_type=F32)
+    return value + lax.dot_general(left[...], right[span, :], NT, preferred_element_type=F32)
+
+
+def exchange(nz, tile, a_hbm, v_hbm, f_hbm, a_buf, right_b, lh_b, ll_b,
+             right_a, lh_a, ll_a, ah, al, v_ref, f_ref, vc, yc, v1, p_buf, rs, y1, yr, sp, srs, szs, sf,
              a_sem, v_sem, f_sem, own_sem, g_send, g1_recv, g2_recv, g3_recv,
-             rs_send, rs_recv, ag_send, ag_recv, ss_send, ss_recv, sg_send, sg_recv, sz_send, sz_recv):
+             rs_send, rs_recv, ag_send, ag_recv, ap_recv, ss_send, ss_recv, sg_send, sg_recv, sz_send, sz_recv):
     row, col = lax.axis_index("row"), lax.axis_index("col")
     z, quad = row // 4, row % 4
     yl, core = quad // 2, quad % 2
@@ -90,16 +97,17 @@
     def hop(index):
         return (index + turn) % nz
 
+    def spread_one(held, which, index):
+        part = held.at[z_rows, :]
+        to = (z + hop(index)) % nz
+
+        @pl.when(to != z)
+        def _():
+            send(part, part, g_send.at[which, 0], g1_recv.at[which, z], to * 4 + quad, col)
+
     def spread(held, which):
-        part = held.at[z_rows, :]
-
         def body(index, carry):
-            to = (z + hop(index)) % nz
-
-            @pl.when(to != z)
-            def _():
-                send(part, part, g_send.at[which, 0], g1_recv.at[which, z], to * 4 + quad, col)
-
+            spread_one(held, which, index)
             return carry
 
         lax.fori_loop(0, nz, body, 0)
@@ -117,7 +125,7 @@
         def _():
             pltpu.make_async_copy(src, dst, g2_recv.at[which, yl]).start()
 
-    def deliver(held, full, which, first, last):
+    def deliver(held, full, which, first, last, following=None):
         def body(index, carry):
             target = (z + nz - hop(index)) % nz
 
@@ -126,6 +134,8 @@
                 drain(held.at[block(target, piece), :], g1_recv.at[which, target])
 
             hand_on(held, full, which, target)
+            if following is not None:
+                spread_one(following, which + 1, index)
             return carry
 
         lax.fori_loop(first, last, body, 0)
@@ -187,33 +197,37 @@
         drain(szs.at[group, 0:nz - 1], sz_send.at[group])
         drain(srs.at[group, 0:plane - 1], sg_send.at[group])
 
-    for panel in range(2):
-        spread(v1.at[panel], panel)
-    va, vb = v_ref[0, mine_rows, :], v_ref[1, mine_rows, :]
-    sp[0, :size] = exact(va, vb, TN)
+    spread(v1.at[0], 0)
+    na, nb = v_ref[0, mine_rows, :], v_ref[1, mine_rows, :]
+    sp[0, :size] = exact(na, nb, TN)
     sp[0, size:] = sp[0, :size]
     sum_start(0)
     load.wait()
     ah[...], al[...] = halves(a_buf[...])
-    deliver(v1.at[0], vc.at[0], 0, 0, nz)
-    deliver(v1.at[1], vc.at[1], 1, 0, nz)
+    deliver(v1.at[0], vc.at[0], 0, 0, nz, v1.at[1])
+    deliver(v1.at[1], vc.at[1], 1, 0, nz // 2)
+    relay(vc.at[0], 0)
+    deliver(v1.at[1], vc.at[1], 1, nz // 2, nz)
     sum_level(0)
 
-    def fold(full, slot, span):
+    rights = (right_a, right_b)
+
+    def fold(full, panel, base, span):
         high, low = halves(full[span, :])
-        right[span, 2 * slot * size:(2 * slot + 1) * size] = high
-        right[span, (2 * slot + 1) * size:(2 * slot + 2) * size] = low
+        rights[panel][span, base:base + size] = high
+        rights[panel][span, base + size:base + 2 * size] = low
 
     for panel in range(2):
-        relay(vc.at[panel], panel)
-        slot = 2 + panel
-        base = 2 * slot * size
+        if panel:
+            relay(vc.at[1], 1)
+            sum_share(0)
+        held = rights[panel]
         for side in range(2):
             partner(vc.at[panel], panel, side)
             span = slice(side * 2 * rows, (side + 1) * 2 * rows)
-            fold(vc.at[panel], slot, span)
-            both = lax.dot_general(ah[:, span], right[span, base:base + 2 * size], NN, preferred_element_type=F32)
-            part = lax.dot_general(al[:, span], right[span, base:base + size], NN, preferred_element_type=F32)
+            fold(vc.at[panel], panel, 2 * size, span)
+            both = lax.dot_general(ah[:, span], held[span, 2 * size:], NN, preferred_element_type=F32)
+            part = lax.dot_general(al[:, span], held[span, 2 * size:3 * size], NN, preferred_element_type=F32)
             part = part + both[:, size:] + both[:, :size]
             p_buf[panel] = part if side == 0 else p_buf[panel] + part
 
@@ -224,9 +238,31 @@
 
         lax.fori_loop(1, nz, scatter, 0)
         rs[panel, mine_rows, :] = p_buf[panel, mine_rows, :]
-    sum_share(0)
-
-    for panel in range(2):
+
+    xn = nz // 2
+    facing = (col + xn) % nz
+
+    def gather_send(panel, owner, with_facing):
+        part = yr.at[panel, block(owner, piece), :]
+        if with_facing:
+            send(part, part, ag_send.at[panel], ap_recv.at[panel], row, facing)
+
+        def body(step, carry):
+            to = (col // xn) * xn + (col + step) % xn
+            send(part, part, ag_send.at[panel], ag_recv.at[panel], row, to)
+            return carry
+
+        lax.fori_loop(1, xn, body, 0)
+
+    def gather_pass(panel):
+        drain(yr.at[panel, block(facing, piece), :], ap_recv.at[panel])
+        gather_send(panel, facing, False)
+
+    def gather_end(panel):
+        if xn > 1:
+            drain(yr.at[panel, 0:2 * (xn - 1) * piece, :], ag_recv.at[panel])
+
+    def reduced(panel):
         drain(rs.at[panel, 0:(nz - 1) * piece, :], rs_recv.at[panel])
         total = rs[panel, 0:piece, :]
         for other in range(1, nz):
@@ -234,40 +270,46 @@
         y1[panel, z_rows, :] = total
         yr[panel, mine_rows, :] = total
         spread(y1.at[panel], 2 + panel)
-        sp[1 + panel, :size] = exact(vb if panel else va, total, TN)
-        sp[1 + panel, size:] = exact(vb, total, TN)
+        sp[1 + panel, :size] = exact(nb if panel else na, total, TN)
+        sp[1 + panel, size:] = exact(nb, total, TN)
         sum_start(1 + panel)
-
-    def gather_all(panel):
-        def body(step, carry):
-            to = (col + step) % nz
-            part = yr.at[panel, mine_rows, :]
-            send(part, part, ag_send.at[panel], ag_recv.at[panel], row, to)
-            return carry
-
-        lax.fori_loop(1, nz, body, 0)
-
-    deliver(y1.at[0], yc.at[0], 2, 0, nz)
-    sum_level(1)
-    gather_all(0)
-    deliver(y1.at[1], yc.at[1], 3, 0, nz)
-    sum_level(2)
-    gather_all(1)
-    sum_share(1)
-    relay(yc.at[0], 2)
-    sum_share(2)
+        gather_send(panel, col, True)
+
+    reduced(0)
 
     load_f.wait()
     f1, f2 = f_ref[0], f_ref[1]
     va, vb = v_ref[0], v_ref[1]
     sum_end(0)
     gram = sf[0, :size]
-    gf = exact(gram, f2)
-    e = exact(f1, gf)
-    lefts = [exact(va, f1, NT) - exact(vb, e, NT), exact(vb, f2, NT)]
-    for panel in range(2):
-        drain(yr.at[panel, 0:(nz - 1) * piece, :], ag_recv.at[panel])
-    ya, yb = yr[0], yr[1]
+    e = exact(f1, exact(gram, f2))
+
+    def keep(high_ref, low_ref, index, value):
+        high, low = halves(value)
+        high_ref[:, 2 * index * size:(2 * index + 1) * size] = high
+        high_ref[:, (2 * index + 1) * size:(2 * index + 2) * size] = high
+        low_ref[:, index * size:(index + 1) * size] = low
+
+    keep(lh_a, ll_a, 0, exact(va, f1, NT) - exact(vb, e, NT))
+    keep(lh_b, ll_b, 0, exact(vb, f2, NT))
+
+    deliver(y1.at[0], yc.at[0], 2, 0, nz // 2)
+    reduced(1)
+    deliver(y1.at[0], yc.at[0], 2, nz // 2, nz)
+    gather_pass(0)
+    sum_level(1)
+    deliver(y1.at[1], yc.at[1], 3, 0, nz // 2)
+    sum_level(2)
+    sum_share(1)
+    deliver(y1.at[1], yc.at[1], 3, nz // 2, nz)
+    gather_pass(1)
+    relay(yc.at[0], 2)
+    sum_share(2)
+    for side in range(2):
+        partner(yc.at[0], 2, side)
+    fold(yc.at[0], 0, 0, slice(0, width))
+    gather_end(0)
+    ya = yr[0]
     sum_end(1)
     s11, s21 = sf[1, :size], sf[1, size:]
     k1 = exact(exact(f1, s11, TN), f1)
@@ -275,22 +317,23 @@
     kg = exact(k1, gram)
     mixed = exact(kg - fs, f2)
     gt = exact(gram, fs - 0.5 * kg, TN)
-    lefts.append(exact(ya, f1) - exact(va, k1) + exact(vb, mixed, NT))
-    rest = exact(yb, f2) - exact(ya, e) + exact(va, mixed)
-    for panel in range(2):
-        if panel:
-            relay(yc.at[1], 3)
-        for side in range(2):
-            partner(yc.at[panel], 2 + panel, side)
-        fold(yc.at[panel], panel, slice(0, width))
+    keep(lh_a, ll_a, 1, exact(ya, f1) - exact(va, k1) + exact(vb, mixed, NT))
+    relay(yc.at[1], 3)
+
+    def first_terms(index, carry):
+        span = pl.ds(pl.multiple_of(index * tile, tile), tile)
+        a_buf[:, span] = a_buf[:, span] - drop(lh_a, ll_a, right_a, span)
+        return carry
+
+    lax.fori_loop(0, width // tile, first_terms, 0)
+    gather_end(1)
+    rest = exact(yr[1], f2) - exact(ya, e) + exact(va, mixed)
+    for side in range(2):
+        partner(yc.at[1], 3, side)
+    fold(yc.at[1], 1, 0, slice(0, width))
     sum_end(2)
     k2 = exact(exact(f2, sf[2, :size] - gt - gt.T, TN), f2)
-    lefts.append(rest - exact(vb, k2))
-    for index, part in enumerate(lefts):
-        high, low = halves(part)
-        lh[:, 2 * index * size:(2 * index + 1) * size] = high
-        lh[:, (2 * index + 1) * size:(2 * index + 2) * size] = high
-        ll[:, index * size:(index + 1) * size] = low
+    keep(lh_b, ll_b, 1, rest - exact(vb, k2))
 
     for panel in range(2):
         settle(v1.at[panel], vc.at[panel], panel)
@@ -301,7 +344,7 @@
         sum_settle(group)
 
 
-def apply_update(tile, size, a_ref, right, lh, ll, out, stage, sems):
+def apply_update(tile, a_ref, right, lh, ll, out, stage, sems):
     count = out.shape[1] // tile
 
     def store(slot, index):
@@ -316,10 +359,7 @@
             store(slot, index - 2).wait()
 
         span = pl.ds(pl.multiple_of(index * tile, tile), tile)
-        highs = jnp.concatenate([right[span, 2 * s * size:(2 * s + 1) * size] for s in range(4)], axis=1)
-        drop = lax.dot_general(ll[...], highs, NT, preferred_element_type=F32)
-        drop = drop + lax.dot_general(lh[...], right[span, :], NT, preferred_element_type=F32)
-        stage[slot] = a_ref[:, span] - drop
+        stage[slot] = a_ref[:, span] - drop(lh, ll, right, span)
         store(slot, index).start()
         return carry
 
@@ -332,6 +372,7 @@
     rows, width = matrix.shape
     size = panels.shape[2]
     srows = 2 * size // (4 * nz)
+    tile = 256 if width % 256 == 0 else width
     vmem = pl.BlockSpec(memory_space=pltpu.VMEM)
     hbm = pl.BlockSpec(memory_space=pltpu.HBM)
     block = pltpu.VMEM((2, rows, size), F32)
@@ -339,29 +380,30 @@
     sums = pltpu.VMEM((3, 2 * size, size), F32)
     dma = pltpu.SemaphoreType.DMA
     held = pl.pallas_call(
-        functools.partial(exchange, nz),
+        functools.partial(exchange, nz, tile),
         out_shape=(
             jax.ShapeDtypeStruct(matrix.shape, F32),
-            jax.ShapeDtypeStruct((width, 8 * size), BF16),
-            jax.ShapeDtypeStruct((rows, 8 * size), BF16),
+            jax.ShapeDtypeStruct((width, 4 * size), BF16),
             jax.ShapeDtypeStruct((rows, 4 * size), BF16),
+            jax.ShapeDtypeStruct((rows, 2 * size), BF16),
         ),
         in_specs=[hbm, hbm, hbm],
         out_specs=(vmem,) * 4,
         scratch_shapes=[
+            pltpu.VMEM((width, 4 * size), BF16), pltpu.VMEM((rows, 4 * size), BF16),
+            pltpu.VMEM((rows, 2 * size), BF16),
             pltpu.VMEM((rows, width), BF16), pltpu.VMEM((rows, width), BF16),
             block, pltpu.VMEM(factors.shape, F32), wide, wide,
             block, block, block, block, block,
             sums, pltpu.VMEM((3, 4 * nz, srows, size), F32),
             pltpu.VMEM((3, nz, srows, size), F32), sums,
             dma(()), dma(()), dma(()), dma(()), dma((4, 5)), dma((4, nz)), dma((4, 2)), dma((4, 2)),
-        ] + [dma((2,))] * 4 + [dma((3,))] * 6,
+        ] + [dma((2,))] * 5 + [dma((3,))] * 6,
         compiler_params=pltpu.CompilerParams(collective_id=0, has_side_effects=True, vmem_limit_bytes=40 << 20),
         name="exchange",
-    )(matrix, panels, factors)
-    tile = 256 if width % 256 == 0 else width
+    )(*(pltpu.with_memory_space_constraint(x, pltpu.HBM) for x in (matrix, panels, factors)))
     return pl.pallas_call(
-        functools.partial(apply_update, tile, size),
+        functools.partial(apply_update, tile),
         out_shape=jax.ShapeDtypeStruct(matrix.shape, F32),
         in_specs=[vmem] * 4,
         out_specs=hbm,

time: 78.3 us -> 72.9 us (0.931)
  local copies, waits for them, and re-layouts: 3.83 us -> 0 us
  Pallas kernels: 74.3 us -> 72.8 us
    unnamed x6 -> x0, local copies, waits for them, and re-layouts: 3.83 us -> none
    pallas_call x2, Pallas kernels: 74.3 us -> 72.8 us  [the longest x1 68.2 us: shards(): pl.pallas_call(functools.partial(exchange, nz, tile), out_shape=(jax.Shap...]
where the time goes in v4:
time: 72.9 us; the launch traced here: 72.8 us
  Pallas kernels  72.8 us (100%)
    pallas_call x1, Pallas kernels, shards(): pl.pallas_call(functools.partial(exchange, nz, tile), out_shape=(jax.Shap...  68.2 us
    pallas_call x1, Pallas kernels, shards(): pl.pallas_call(functools.partial(apply_update, tile), out_shape=jax.Shape...  4.59 us

profile of v4, /device:TPU:1, one launch (start us, length us, event | category | flops | bytes accessed | tf_op | source)
XLA Modules:
  0.0 72.8 jit_solution(10804618182470168684)
XLA Ops:
  0.0 68.2 %exchange.1 = (f32[448,1792]{1,0:T(8,128)S(1)}, bf16[1792,512]{1,0:T(8,128)(2,1)S(1)}, bf16[448,512]{1,0:T(8,128)(2,1)S(1)}, bf16[448,256]{1,0:T(8,128)(2,1)S(1)}) custom-call(f32[448,1792]{1,0:T(8,128)} %a_hbm.1, f32[2,448,128]{2,1,0:T(8,128)} %v_hbm.1, f32[2,128,128]{2,1,0:T(8,128)} %f_hbm.1), custom_call_target="tpu_custom_call" | custom-call | tf_op jit(solution)/shard_map/exchange/pallas_call | solution.py:382
  68.2 4.6 %apply_update.1 = f32[448,1792]{1,0:T(8,128)} custom-call(f32[448,1792]{1,0:T(8,128)S(1)} %get-tuple-element.9.a_ref, bf16[1792,512]{1,0:T(8,128)(2,1)S(1)} %get-tuple-element.10.right, bf16[448,512]{1,0:T(8,128)(2,1)S(1)} %get-tuple-element.11.lh, bf16[448,256]{1,0:T(8,128)(2,1)S(1)} %get-tuple-element.12.ll), custom_call_target="tpu_custom_call" | custom-call | tf_op jit(solution)/shard_map/apply_update/pallas_call | solution.py:405

commit v5 on v4

--- a/solution.py
+++ b/solution.py
@@ -92,7 +92,7 @@
     own.wait()
     pl.semaphore_wait(barrier, nz - 1 + plane - 1)
 
-    turn = col + 2 * quad
+    turn = col + 4 * core
 
     def hop(index):
         return (index + turn) % nz
@@ -294,22 +294,24 @@
     keep(lh_b, ll_b, 0, exact(vb, f2, NT))
 
     deliver(y1.at[0], yc.at[0], 2, 0, nz // 2)
+    sum_level(1)
     reduced(1)
     deliver(y1.at[0], yc.at[0], 2, nz // 2, nz)
     gather_pass(0)
-    sum_level(1)
+    sum_share(1)
     deliver(y1.at[1], yc.at[1], 3, 0, nz // 2)
     sum_level(2)
-    sum_share(1)
     deliver(y1.at[1], yc.at[1], 3, nz // 2, nz)
+    relay(yc.at[0], 2)
+    gather_end(0)
+    ya = yr[0]
+    most = exact(ya, f1)
+    crossed = exact(ya, e)
+    sum_share(2)
     gather_pass(1)
-    relay(yc.at[0], 2)
-    sum_share(2)
     for side in range(2):
         partner(yc.at[0], 2, side)
     fold(yc.at[0], 0, 0, slice(0, width))
-    gather_end(0)
-    ya = yr[0]
     sum_end(1)
     s11, s21 = sf[1, :size], sf[1, size:]
     k1 = exact(exact(f1, s11, TN), f1)
@@ -317,8 +319,7 @@
     kg = exact(k1, gram)
     mixed = exact(kg - fs, f2)
     gt = exact(gram, fs - 0.5 * kg, TN)
-    keep(lh_a, ll_a, 1, exact(ya, f1) - exact(va, k1) + exact(vb, mixed, NT))
-    relay(yc.at[1], 3)
+    keep(lh_a, ll_a, 1, most - exact(va, k1) + exact(vb, mixed, NT))
 
     def first_terms(index, carry):
         span = pl.ds(pl.multiple_of(index * tile, tile), tile)
@@ -326,8 +327,9 @@
         return carry
 
     lax.fori_loop(0, width // tile, first_terms, 0)
+    relay(yc.at[1], 3)
     gather_end(1)
-    rest = exact(yr[1], f2) - exact(ya, e) + exact(va, mixed)
+    rest = exact(yr[1], f2) - crossed + exact(va, mixed)
     for side in range(2):
         partner(yc.at[1], 3, side)
     fold(yc.at[1], 1, 0, slice(0, width))

time: 72.9 us -> 69.5 us (0.953)
  Pallas kernels: 72.8 us -> 69.4 us
    pallas_call x1, Pallas kernels: 68.2 us -> 64.9 us  [shards(): pl.pallas_call(functools.partial(exchange, nz, tile), out_shape=(jax.Shap...]
where the time goes in v5:
time: 69.5 us
  Pallas kernels  69.4 us (100%)
    pallas_call x1, Pallas kernels, shards(): pl.pallas_call(functools.partial(exchange, nz, tile), out_shape=(jax.Shap...  64.9 us
    pallas_call x1, Pallas kernels, shards(): pl.pallas_call(functools.partial(apply_update, tile), out_shape=jax.Shape...  4.59 us

profile of v5, /device:TPU:1, one launch (start us, length us, event | category | flops | bytes accessed | tf_op | source)
XLA Modules:
  0.0 69.5 jit_solution(2305909224885346395)
XLA Ops:
  0.0 64.9 %exchange.1 = (f32[448,1792]{1,0:T(8,128)S(1)}, bf16[1792,512]{1,0:T(8,128)(2,1)S(1)}, bf16[448,512]{1,0:T(8,128)(2,1)S(1)}, bf16[448,256]{1,0:T(8,128)(2,1)S(1)}) custom-call(f32[448,1792]{1,0:T(8,128)} %a_hbm.1, f32[2,448,128]{2,1,0:T(8,128)} %v_hbm.1, f32[2,128,128]{2,1,0:T(8,128)} %f_hbm.1), custom_call_target="tpu_custom_call" | custom-call | tf_op jit(solution)/shard_map/exchange/pallas_call | solution.py:384
  64.9 4.6 %apply_update.1 = f32[448,1792]{1,0:T(8,128)} custom-call(f32[448,1792]{1,0:T(8,128)S(1)} %get-tuple-element.9.a_ref, bf16[1792,512]{1,0:T(8,128)(2,1)S(1)} %get-tuple-element.10.right, bf16[448,512]{1,0:T(8,128)(2,1)S(1)} %get-tuple-element.11.lh, bf16[448,256]{1,0:T(8,128)(2,1)S(1)} %get-tuple-element.12.ll), custom_call_target="tpu_custom_call" | custom-call | tf_op jit(solution)/shard_map/apply_update/pallas_call | solution.py:407

commit v6 on v5

--- a/solution.py
+++ b/solution.py
@@ -156,51 +156,90 @@
         for side in range(2):
             drain(full.at[0:rows, :], g_send.at[which, 3 + side])
 
+    def own_rows(group):
+        return s_rows if group == 1 else block(mine // 2, srows)
+
+    def if_owner(group):
+        return pl.when(core == 0) if group != 1 else (lambda body: body())
+
     def sum_start(group):
-        def body(step, carry):
-            to_row, to_col = ppeer(step)
-            other = (mine + step) % plane
-            send(sp.at[group, block(other, srows), :], srs.at[group, mine], ss_send.at[group], ss_recv.at[group], to_row, to_col)
-            return carry
-
-        lax.fori_loop(1, plane, body, 0)
-        srs[group, mine] = sp[group, s_rows, :]
+        if group == 1:
+            def body(step, carry):
+                to_row, to_col = ppeer(step)
+                other = (mine + step) % plane
+                send(sp.at[group, block(other, srows), :], srs.at[group, mine], ss_send.at[group], ss_recv.at[group], to_row, to_col)
+                return carry
+
+            lax.fori_loop(1, plane, body, 0)
+        else:
+            def body(step, carry):
+                owner = (mine // 2 + step) % (plane // 2)
+
+                @pl.when((step > 0) | (core == 1))
+                def _():
+                    send(sp.at[group, block(owner, srows), :], srs.at[group, mine], ss_send.at[group], ss_recv.at[group], z * 4 + (owner % 2) * 2, owner // 2)
+
+                return carry
+
+            lax.fori_loop(0, plane // 2, body, 0)
+
+        @if_owner(group)
+        def _():
+            srs[group, mine] = sp[group, own_rows(group), :]
 
     def sum_level(group):
-        drain(srs.at[group, 0:plane - 1], ss_recv.at[group])
-        szs[group, z] = jnp.sum(srs[group], axis=0)
-
-        def body(step, carry):
-            part = szs.at[group, z]
-            send(part, part, sz_send.at[group], sz_recv.at[group], zpeer(step) * 4 + quad, col)
-            return carry
-
-        lax.fori_loop(1, nz, body, 0)
+        @if_owner(group)
+        def _():
+            drain(srs.at[group, 0:plane - 1], ss_recv.at[group])
+            szs[group, z] = jnp.sum(srs[group], axis=0)
+
+            def body(step, carry):
+                part = szs.at[group, z]
+                send(part, part, sz_send.at[group], sz_recv.at[group], zpeer(step) * 4 + quad, col)
+                return carry
+
+            lax.fori_loop(1, nz, body, 0)
 
     def sum_share(group):
-        drain(szs.at[group, 0:nz - 1], sz_recv.at[group])
-        sf[group, s_rows, :] = jnp.sum(szs[group], axis=0)
-
-        def body(step, carry):
-            to_row, to_col = ppeer(step)
-            part = sf.at[group, s_rows, :]
-            send(part, part, sg_send.at[group], sg_recv.at[group], to_row, to_col)
-            return carry
-
-        lax.fori_loop(1, plane, body, 0)
+        @if_owner(group)
+        def _():
+            drain(szs.at[group, 0:nz - 1], sz_recv.at[group])
+            sf[group, own_rows(group), :] = jnp.sum(szs[group], axis=0)
+
+            def body(step, carry):
+                to_row, to_col = ppeer(step)
+                part = sf.at[group, own_rows(group), :]
+                send(part, part, sg_send.at[group], sg_recv.at[group], to_row, to_col)
+                return carry
+
+            lax.fori_loop(1, plane, body, 0)
+
+    def drain_others(ref, sem):
+        for parity in range(2):
+            @pl.when(core == parity)
+            def _(parity=parity):
+                drain(ref.at[0:(plane // 2 - 1 + parity) * srows, :], sem)
 
     def sum_end(group):
-        drain(sf.at[group, 0:(plane - 1) * srows, :], sg_recv.at[group])
+        if group == 1:
+            drain(sf.at[group, 0:(plane - 1) * srows, :], sg_recv.at[group])
+        else:
+            drain_others(sf.at[group], sg_recv.at[group])
 
     def sum_settle(group):
-        drain(srs.at[group, 0:plane - 1], ss_send.at[group])
-        drain(szs.at[group, 0:nz - 1], sz_send.at[group])
-        drain(srs.at[group, 0:plane - 1], sg_send.at[group])
+        if group == 1:
+            drain(srs.at[group, 0:plane - 1], ss_send.at[group])
+        else:
+            drain_others(sf.at[group], ss_send.at[group])
+
+        @if_owner(group)
+        def _():
+            drain(szs.at[group, 0:nz - 1], sz_send.at[group])
+            drain(srs.at[group, 0:plane - 1], sg_send.at[group])
 
     spread(v1.at[0], 0)
     na, nb = v_ref[0, mine_rows, :], v_ref[1, mine_rows, :]
     sp[0, :size] = exact(na, nb, TN)
-    sp[0, size:] = sp[0, :size]
     sum_start(0)
     load.wait()
     ah[...], al[...] = halves(a_buf[...])
@@ -271,7 +310,8 @@
         yr[panel, mine_rows, :] = total
         spread(y1.at[panel], 2 + panel)
         sp[1 + panel, :size] = exact(nb if panel else na, total, TN)
-        sp[1 + panel, size:] = exact(nb, total, TN)
+        if panel == 0:
+            sp[1, size:] = exact(nb, total, TN)
         sum_start(1 + panel)
         gather_send(panel, col, True)
 
@@ -326,7 +366,9 @@
         a_buf[:, span] = a_buf[:, span] - drop(lh_a, ll_a, right_a, span)
         return carry
 
-    lax.fori_loop(0, width // tile, first_terms, 0)
+    for index in range(0, width, 256):
+        span = slice(index, index + 256)
+        a_buf[:, span] = a_buf[:, span] - drop(lh_a, ll_a, right_a, span)
     relay(yc.at[1], 3)
     gather_end(1)
     rest = exact(yr[1], f2) - crossed + exact(va, mixed)
@@ -347,34 +389,23 @@
 
 
 def apply_update(tile, a_ref, right, lh, ll, out, stage, sems):
-    count = out.shape[1] // tile
-
-    def store(slot, index):
-        span = pl.ds(pl.multiple_of(index * tile, tile), tile)
-        return pltpu.make_async_copy(stage.at[slot], out.at[:, span], sems.at[slot])
-
-    def body(index, carry):
-        slot = index % 2
-
-        @pl.when(index >= 2)
-        def _():
-            store(slot, index - 2).wait()
-
-        span = pl.ds(pl.multiple_of(index * tile, tile), tile)
-        stage[slot] = a_ref[:, span] - drop(lh, ll, right, span)
-        store(slot, index).start()
-        return carry
-
-    lax.fori_loop(0, count, body, 0)
-    for index in range(max(count - 2, 0), count):
-        store(index % 2, index).wait()
+    width = out.shape[1]
+    ends = list(range(512, width, 512))
+    stores = []
+    for index, (start, stop) in enumerate(zip([0] + ends, ends + [width])):
+        span = slice(start, stop)
+        stage[:, span] = a_ref[:, span] - drop(lh, ll, right, span)
+        stores.append(pltpu.make_async_copy(stage.at[:, span], out.at[:, span], sems.at[index]))
+        stores[-1].start()
+    for store in stores:
+        store.wait()
 
 
 def shards(nz, matrix, panels, factors):
     rows, width = matrix.shape
     size = panels.shape[2]
     srows = 2 * size // (4 * nz)
-    tile = 256 if width % 256 == 0 else width
+    tile = 896 if width % 896 == 0 else width
     vmem = pl.BlockSpec(memory_space=pltpu.VMEM)
     hbm = pl.BlockSpec(memory_space=pltpu.HBM)
     block = pltpu.VMEM((2, rows, size), F32)
@@ -409,7 +440,7 @@
         out_shape=jax.ShapeDtypeStruct(matrix.shape, F32),
         in_specs=[vmem] * 4,
         out_specs=hbm,
-        scratch_shapes=[pltpu.VMEM((2, rows, tile), F32), dma((2,))],
+        scratch_shapes=[pltpu.VMEM((rows, width), F32), dma((8,))],
         compiler_params=pltpu.CompilerParams(vmem_limit_bytes=24 << 20),
         name="apply_update",
     )(*held)

time: 69.5 us -> 65.7 us (0.945)
  Pallas kernels: 69.4 us -> 65.6 us
    pallas_call x1, Pallas kernels: 4.59 us -> 2.54 us  [shards(): pl.pallas_call(functools.partial(apply_update, tile), out_shape=jax.Shape...]
    pallas_call x1, Pallas kernels: 64.9 us -> 63.1 us  [shards(): pl.pallas_call(functools.partial(exchange, nz, tile), out_shape=(jax.Shap...]
where the time goes in v6:
time: 65.7 us; the launch traced here: 65.6 us
  Pallas kernels  65.6 us (100%)
    pallas_call x1, Pallas kernels, shards(): pl.pallas_call(functools.partial(exchange, nz, tile), out_shape=(jax.Shap...  63.1 us
    pallas_call x1, Pallas kernels, shards(): pl.pallas_call(functools.partial(apply_update, tile), out_shape=jax.Shape...  2.54 us

profile of v6, /device:TPU:1, one launch (start us, length us, event | category | flops | bytes accessed | tf_op | source)
XLA Modules:
  0.0 65.6 jit_solution(14540971548810589080)
XLA Ops:
  0.0 63.1 %exchange.1 = (f32[448,1792]{1,0:T(8,128)S(1)}, bf16[1792,512]{1,0:T(8,128)(2,1)S(1)}, bf16[448,512]{1,0:T(8,128)(2,1)S(1)}, bf16[448,256]{1,0:T(8,128)(2,1)S(1)}) custom-call(f32[448,1792]{1,0:T(8,128)} %a_hbm.1, f32[2,448,128]{2,1,0:T(8,128)} %v_hbm.1, f32[2,128,128]{2,1,0:T(8,128)} %f_hbm.1), custom_call_target="tpu_custom_call" | custom-call | tf_op jit(solution)/shard_map/exchange/pallas_call | solution.py:415
  63.1 2.5 %apply_update.1 = f32[448,1792]{1,0:T(8,128)} custom-call(f32[448,1792]{1,0:T(8,128)S(1)} %get-tuple-element.9.a_ref, bf16[1792,512]{1,0:T(8,128)(2,1)S(1)} %get-tuple-element.10.right, bf16[448,512]{1,0:T(8,128)(2,1)S(1)} %get-tuple-element.11.lh, bf16[448,256]{1,0:T(8,128)(2,1)S(1)} %get-tuple-element.12.ll), custom_call_target="tpu_custom_call" | custom-call | tf_op jit(solution)/shard_map/apply_update/pallas_call | solution.py:438

commit v7 on v6

--- a/solution.py
+++ b/solution.py
@@ -263,12 +263,10 @@
         held = rights[panel]
         for side in range(2):
             partner(vc.at[panel], panel, side)
-            span = slice(side * 2 * rows, (side + 1) * 2 * rows)
-            fold(vc.at[panel], panel, 2 * size, span)
-            both = lax.dot_general(ah[:, span], held[span, 2 * size:], NN, preferred_element_type=F32)
-            part = lax.dot_general(al[:, span], held[span, 2 * size:3 * size], NN, preferred_element_type=F32)
-            part = part + both[:, size:] + both[:, :size]
-            p_buf[panel] = part if side == 0 else p_buf[panel] + part
+        fold(vc.at[panel], panel, 2 * size, slice(0, width))
+        both = lax.dot_general(ah[...], held[:, 2 * size:], NN, preferred_element_type=F32)
+        part = lax.dot_general(al[...], held[:, 2 * size:3 * size], NN, preferred_element_type=F32)
+        p_buf[panel] = part + both[:, size:] + both[:, :size]
 
         def scatter(step, carry, panel=panel):
             to = (col + step) % nz
@@ -372,13 +370,13 @@
     relay(yc.at[1], 3)
     gather_end(1)
     rest = exact(yr[1], f2) - crossed + exact(va, mixed)
+    sum_end(2)
+    k2 = exact(exact(f2, sf[2, :size] - gt - gt.T, TN), f2)
+    keep(lh_b, ll_b, 1, rest - exact(vb, k2))
+
     for side in range(2):
         partner(yc.at[1], 3, side)
     fold(yc.at[1], 1, 0, slice(0, width))
-    sum_end(2)
-    k2 = exact(exact(f2, sf[2, :size] - gt - gt.T, TN), f2)
-    keep(lh_b, ll_b, 1, rest - exact(vb, k2))
-
     for panel in range(2):
         settle(v1.at[panel], vc.at[panel], panel)
         settle(y1.at[panel], yc.at[panel], 2 + panel)

time: 65.7 us -> 65.7 us (level)
  no operation moved by 1% of the time
where the time goes in v7:
time: 65.7 us; the launch traced here: 65.6 us
  Pallas kernels  65.6 us (100%)
    pallas_call x1, Pallas kernels, shards(): pl.pallas_call(functools.partial(exchange, nz, tile), out_shape=(jax.Shap...  63.1 us
    pallas_call x1, Pallas kernels, shards(): pl.pallas_call(functools.partial(apply_update, tile), out_shape=jax.Shape...  2.53 us

profile of v7, /device:TPU:1, one launch (start us, length us, event | category | flops | bytes accessed | tf_op | source)
XLA Modules:
  0.0 65.6 jit_solution(11944438257252925916)
XLA Ops:
  0.0 63.1 %exchange.1 = (f32[448,1792]{1,0:T(8,128)S(1)}, bf16[1792,512]{1,0:T(8,128)(2,1)S(1)}, bf16[448,512]{1,0:T(8,128)(2,1)S(1)}, bf16[448,256]{1,0:T(8,128)(2,1)S(1)}) custom-call(f32[448,1792]{1,0:T(8,128)} %a_hbm.1, f32[2,448,128]{2,1,0:T(8,128)} %v_hbm.1, f32[2,128,128]{2,1,0:T(8,128)} %f_hbm.1), custom_call_target="tpu_custom_call" | custom-call | tf_op jit(solution)/shard_map/exchange/pallas_call | solution.py:413
  63.1 2.5 %apply_update.1 = f32[448,1792]{1,0:T(8,128)} custom-call(f32[448,1792]{1,0:T(8,128)S(1)} %get-tuple-element.9.a_ref, bf16[1792,512]{1,0:T(8,128)(2,1)S(1)} %get-tuple-element.10.right, bf16[448,512]{1,0:T(8,128)(2,1)S(1)} %get-tuple-element.11.lh, bf16[448,256]{1,0:T(8,128)(2,1)S(1)} %get-tuple-element.12.ll), custom_call_target="tpu_custom_call" | custom-call | tf_op jit(solution)/shard_map/apply_update/pallas_call | solution.py:436
